TPU v7x, 32 devices: a whole 2x2x4 slice. The times are simulated.
32 devices in a mesh: dp: 8 (over y, x, core), mp: 4 (over z).
Axes of the slice: x: 2, y: 2, z: 4, core: 2. Of those that a mesh axis runs over, the one named last changes fastest.
Arguments:
- inputs: bfloat16 [8192, 2048], P('dp'), may hold values from -6 to 6
- segments: int32 [8192], P('dp'), may hold values from 0 to 511, as said below
- padding: int32 [8192], P('dp'), may hold values from 0 to 1, as said below
- first_gain: bfloat16 [2048], P('dp'), may hold values from 0.5 to 1.5
- first_shift: bfloat16 [2048], P('dp'), may hold values from -4 to 4
- second_gain: bfloat16 [2048], P('dp'), may hold values from 0.5 to 1.5
- second_shift: bfloat16 [2048], P('dp'), may hold values from -4 to 4
- joint_weight: bfloat16 [2048, 6144], P('dp', 'mp'), may hold values from -1 to 1
- joint_bias: bfloat16 [6144], P(('mp', 'dp')), may hold values from -4 to 4
- dense_weight: bfloat16 [2048, 2048], P('mp', 'dp'), may hold values from -0.75 to 0.75
- dense_bias: bfloat16 [2048], P('dp'), may hold values from -4 to 4
- expand_weight: bfloat16 [2048, 8192], P('dp', 'mp'), may hold values from -0.125 to 0.125
- expand_bias: bfloat16 [8192], P(('mp', 'dp')), may hold values from -6 to 6
- reduce_weight: bfloat16 [8192, 2048], P('mp', 'dp'), may hold values from -0.0625 to 0.0625
- reduce_bias: bfloat16 [2048], P('dp'), may hold values from -4 to 4
- cotangent: bfloat16 [8192, 2048], P('dp'), may hold values from -6 to 6
Outputs:
- result: bfloat16 [8192, 2048], P('dp')
- inputs_back: bfloat16 [8192, 2048], P('dp')
- first_gain_back: float32 [2048], P('dp')
- first_shift_back: float32 [2048], P('dp')
- second_gain_back: float32 [2048], P('dp')
- second_shift_back: float32 [2048], P('dp')
- joint_weight_back: float32 [2048, 6144], P('dp', 'mp')
- joint_bias_back: float32 [6144], P(('mp', 'dp'))
- dense_weight_back: float32 [2048, 2048], P('mp', 'dp')
- dense_bias_back: float32 [2048], P('dp')
- expand_weight_back: float32 [2048, 8192], P('dp', 'mp')
- expand_bias_back: float32 [8192], P(('mp', 'dp'))
- reduce_weight_back: float32 [8192, 2048], P('mp', 'dp')
- reduce_bias_back: float32 [2048], P('dp')
Inputs may be any that keep to these rules, and one draw needn't show every extreme that they name: `segments`: within each aligned block of 512 rows the ids never fall from row to row; a block ends with 1 to 384 padding rows that carry the id 512 - 1, and its sequences carry smaller ids; no sequence crosses a block's end. 0 exactly on the padding rows that end each block of 512 rows.
All inputs are finite; a program needn't handle non-finite values.
Results may differ from a plain program's by a relative error of at most 0.018.
Values may be sent and summed in bfloat16 or wider, within the bound.
No kernel may reach another device: no remote copies, remote signals or barrier semaphores. Data moves between devices by JAX's collectives and lax.ppermute only.
A program may use at most 256 MiB of HBM per device.

v0:
```python
import math

import jax
import jax.numpy as jnp
from jax import lax
from jax.sharding import PartitionSpec as P

HD = 256
ROT = 64
MICRO = 2


EPS = 1e-05
NEGATIVE = -1e30
ROOT_HALF = 0.7071067811865476
ROOT_TWOPI = 2.5066282746310002


def normalize(matrix):
    centred = matrix - jnp.mean(matrix, axis=1, keepdims=True)
    scale_inv = lax.rsqrt(jnp.mean(centred * centred, axis=1, keepdims=True) + EPS)
    return (centred * scale_inv, scale_inv)


def layout(labels):
    indices = jnp.arange(labels.shape[0])
    matching = labels[:, None] == labels[None, :]
    earlier = indices[None, :] < indices[:, None]
    positions = jnp.sum((matching & earlier).astype(jnp.int32), axis=1).astype(jnp.float32)
    allowed = matching & (indices[None, :] <= indices[:, None])
    return (positions, allowed)


def rotary_tables(positions):
    half_width = ROT // 2
    frequency = jnp.exp(
        jnp.arange(half_width, dtype=jnp.float32) * (-2.0 * math.log(10000.0) / ROT)
    )
    angles = positions[:, None] * frequency[None, :]
    return (jnp.cos(angles)[:, None, :], jnp.sin(angles)[:, None, :])


def rotate(tensor, cosine_table, sine_table):
    half_width = ROT // 2
    leading = tensor[..., :half_width]
    trailing = tensor[..., half_width:ROT]
    remain = tensor[..., ROT:]
    return jnp.concatenate(
        [
            leading * cosine_table - trailing * sine_table,
            trailing * cosine_table + leading * sine_table,
            remain,
        ],
        axis=-1,
    )


def unrotate(tensor, cosine_table, sine_table):
    half_width = ROT // 2
    leading = tensor[..., :half_width]
    trailing = tensor[..., half_width:ROT]
    remain = tensor[..., ROT:]
    return jnp.concatenate(
        [
            leading * cosine_table + trailing * sine_table,
            trailing * cosine_table - leading * sine_table,
            remain,
        ],
        axis=-1,
    )


def gelu_value(values):
    return 0.5 * values * (1.0 + lax.erf(values * ROOT_HALF))


def gelu_slope(values):
    return (
        0.5 * (1.0 + lax.erf(values * ROOT_HALF))
        + values * jnp.exp(-0.5 * values * values) / ROOT_TWOPI
    )


def attend_forward(queries, key_rows, value_rows, allowed):
    total_rows, head_count, head_depth = queries.shape
    block_rows = min(512, total_rows)
    block_count = total_rows // block_rows

    def one_block(pieces):
        query_block, mask_block = pieces
        scores = jnp.einsum(
            "qhd,khd->hqk", query_block, key_rows, preferred_element_type=jnp.float32
        )
        scores = jnp.where(mask_block[None], scores, NEGATIVE)
        row_peak = jnp.max(scores, axis=2, keepdims=True)
        logsum = row_peak + jnp.log(jnp.sum(jnp.exp(scores - row_peak), axis=2, keepdims=True))
        weights = jnp.exp(scores - logsum).astype(jnp.bfloat16)
        mixture = jnp.einsum(
            "hqk,khd->qhd", weights, value_rows, preferred_element_type=jnp.float32
        )
        return (mixture.astype(jnp.bfloat16), logsum[:, :, 0])

    blocks = (
        queries.reshape(block_count, block_rows, head_count, head_depth),
        allowed.reshape(block_count, block_rows, total_rows),
    )
    mixture, logsum = lax.map(one_block, blocks)
    return (mixture.reshape(total_rows, head_count, head_depth), logsum)


def attend_backward(queries, key_rows, value_rows, mixture, grad_mixture, allowed, logsum):
    total_rows, head_count, head_depth = queries.shape
    block_rows = min(512, total_rows)
    block_count = total_rows // block_rows

    def one_block(running, pieces):
        key_grad, value_grad = running
        query_block, mixture_block, grad_block, mask_block, logsum_block = pieces
        scores = jnp.einsum(
            "qhd,khd->hqk", query_block, key_rows, preferred_element_type=jnp.float32
        )
        scores = jnp.where(mask_block[None], scores, NEGATIVE)
        chances = jnp.exp(scores - logsum_block[:, :, None])
        weights = chances.astype(jnp.bfloat16)
        value_grad = value_grad + jnp.einsum(
            "hqk,qhd->khd", weights, grad_block, preferred_element_type=jnp.float32
        )
        weight_grad = jnp.einsum(
            "qhd,khd->hqk", grad_block, value_rows, preferred_element_type=jnp.float32
        )
        row_dot = jnp.sum(
            grad_block.astype(jnp.float32) * mixture_block.astype(jnp.float32), axis=2
        ).T
        score_grad = (chances * (weight_grad - row_dot[:, :, None])).astype(jnp.bfloat16)
        query_grad = jnp.einsum(
            "hqk,khd->qhd", score_grad, key_rows, preferred_element_type=jnp.float32
        )
        key_grad = key_grad + jnp.einsum(
            "hqk,qhd->khd", score_grad, query_block, preferred_element_type=jnp.float32
        )
        return ((key_grad, value_grad), query_grad)

    empty = jnp.zeros((total_rows, head_count, head_depth), jnp.float32)
    pieces = (
        queries.reshape(block_count, block_rows, head_count, head_depth),
        mixture.reshape(block_count, block_rows, head_count, head_depth),
        grad_mixture.reshape(block_count, block_rows, head_count, head_depth),
        allowed.reshape(block_count, block_rows, total_rows),
        logsum,
    )
    (key_grad, value_grad), query_grad = lax.scan(one_block, (empty, empty), pieces)
    return (query_grad.reshape(total_rows, head_count, head_depth), key_grad, value_grad)


def shards(
    inputs,
    segments,
    padding,
    first_gain,
    first_shift,
    second_gain,
    second_shift,
    joint_weight,
    joint_bias,
    dense_weight,
    dense_bias,
    expand_weight,
    expand_bias,
    reduce_weight,
    reduce_bias,
    cotangent,
):
    local_rows = inputs.shape[0] // MICRO
    head_count = joint_weight.shape[1] // (3 * HD)
    query_scale = HD ** (-0.5)
    totals = None
    outputs = []
    back_rows = []
    for micro_index in range(MICRO):
        row_start = micro_index * local_rows
        row_stop = row_start + local_rows
        forward_set = (
            lax.all_gather(joint_weight, "dp", axis=0, tiled=True),
            lax.all_gather(joint_bias, "dp", axis=0, tiled=True),
            lax.all_gather(dense_weight, "dp", axis=1, tiled=True),
            lax.all_gather(dense_bias, "dp", axis=0, tiled=True),
            lax.all_gather(expand_weight, "dp", axis=0, tiled=True),
            lax.all_gather(expand_bias, "dp", axis=0, tiled=True),
            lax.all_gather(reduce_weight, "dp", axis=1, tiled=True),
            lax.all_gather(reduce_bias, "dp", axis=0, tiled=True),
            lax.all_gather(first_gain, "dp", axis=0, tiled=True),
            lax.all_gather(first_shift, "dp", axis=0, tiled=True),
            lax.all_gather(second_gain, "dp", axis=0, tiled=True),
            lax.all_gather(second_shift, "dp", axis=0, tiled=True),
        )
        (
            joint_full,
            joint_bias_full,
            dense_full,
            dense_bias_full,
            expand_full,
            expand_bias_full,
            reduce_full,
            reduce_bias_full,
            gain_one,
            shift_one,
            gain_two,
            shift_two,
        ) = forward_set
        rows_in = inputs[row_start:row_stop].astype(jnp.float32)
        normed, scale_inv = normalize(rows_in)
        hidden_one = (normed * gain_one.astype(jnp.float32) + shift_one.astype(jnp.float32)).astype(
            jnp.bfloat16
        )
        hidden_two = (normed * gain_two.astype(jnp.float32) + shift_two.astype(jnp.float32)).astype(
            jnp.bfloat16
        )
        positions, allowed = layout(segments[row_start:row_stop])
        cosine_table, sine_table = rotary_tables(positions)
        joint = (
            jnp.dot(hidden_one, joint_full, preferred_element_type=jnp.float32)
            + joint_bias_full.astype(jnp.float32)
        ).reshape(local_rows, head_count, 3, HD)
        queries = (rotate(joint[:, :, 0], cosine_table, sine_table) * query_scale).astype(
            jnp.bfloat16
        )
        key_rows = rotate(joint[:, :, 1], cosine_table, sine_table).astype(jnp.bfloat16)
        value_rows = joint[:, :, 2].astype(jnp.bfloat16)
        mixture, logsum = attend_forward(queries, key_rows, value_rows, allowed)
        mixture_flat = mixture.reshape(local_rows, head_count * HD)
        before = jnp.dot(
            hidden_two, expand_full, preferred_element_type=jnp.float32
        ) + expand_bias_full.astype(jnp.float32)
        activated = gelu_value(before).astype(jnp.bfloat16)
        branch_part = jnp.dot(
            mixture_flat, dense_full, preferred_element_type=jnp.float32
        ) + jnp.dot(activated, reduce_full, preferred_element_type=jnp.float32)
        branches = lax.psum(branch_part.astype(jnp.bfloat16), "mp").astype(jnp.float32)
        outputs.append(
            (
                rows_in
                + branches
                + dense_bias_full.astype(jnp.float32)
                + reduce_bias_full.astype(jnp.float32)
            ).astype(jnp.bfloat16)
        )
        joint_again, dense_again, expand_again, reduce_again, first_again, second_again = (
            lax.all_gather(joint_weight, "dp", axis=0, tiled=True),
            lax.all_gather(dense_weight, "dp", axis=1, tiled=True),
            lax.all_gather(expand_weight, "dp", axis=0, tiled=True),
            lax.all_gather(reduce_weight, "dp", axis=1, tiled=True),
            lax.all_gather(first_gain, "dp", axis=0, tiled=True),
            lax.all_gather(second_gain, "dp", axis=0, tiled=True),
        )
        seed_grad = (
            cotangent[row_start:row_stop].astype(jnp.float32)
            * padding[row_start:row_stop].astype(jnp.float32)[:, None]
        )
        seed_low = seed_grad.astype(jnp.bfloat16)
        bias_grad = jnp.sum(seed_grad, axis=0)
        grad_mixture = (
            jnp.dot(seed_low, dense_again.T, preferred_element_type=jnp.float32)
            .astype(jnp.bfloat16)
            .reshape(local_rows, head_count, HD)
        )
        before_grad = jnp.dot(
            seed_low, reduce_again.T, preferred_element_type=jnp.float32
        ) * gelu_slope(before)
        before_low = before_grad.astype(jnp.bfloat16)
        query_grad, key_grad, value_grad = attend_backward(
            queries, key_rows, value_rows, mixture, grad_mixture, allowed, logsum
        )
        joint_grad = jnp.stack(
            [
                unrotate(query_grad * query_scale, cosine_table, sine_table),
                unrotate(key_grad, cosine_table, sine_table),
                value_grad,
            ],
            axis=2,
        ).reshape(local_rows, 3 * head_count * HD)
        joint_low = joint_grad.astype(jnp.bfloat16)
        grad_one, grad_two = (
            lax.psum(
                jnp.dot(joint_low, joint_again.T, preferred_element_type=jnp.float32).astype(
                    jnp.bfloat16
                ),
                "mp",
            ).astype(jnp.float32),
            lax.psum(
                jnp.dot(before_low, expand_again.T, preferred_element_type=jnp.float32).astype(
                    jnp.bfloat16
                ),
                "mp",
            ).astype(jnp.float32),
        )
        grad_normed = grad_one * first_again.astype(jnp.float32) + grad_two * second_again.astype(
            jnp.float32
        )
        back_rows.append(
            (
                seed_grad
                + scale_inv
                * (
                    grad_normed
                    - jnp.mean(grad_normed, axis=1, keepdims=True)
                    - normed * jnp.mean(grad_normed * normed, axis=1, keepdims=True)
                )
            ).astype(jnp.bfloat16)
        )
        terms = (
            jnp.sum(grad_one * normed, axis=0),
            jnp.sum(grad_one, axis=0),
            jnp.sum(grad_two * normed, axis=0),
            jnp.sum(grad_two, axis=0),
            jnp.dot(hidden_one.T, joint_low, preferred_element_type=jnp.float32),
            jnp.sum(joint_grad, axis=0),
            jnp.dot(mixture_flat.T, seed_low, preferred_element_type=jnp.float32),
            bias_grad,
            jnp.dot(hidden_two.T, before_low, preferred_element_type=jnp.float32),
            jnp.sum(before_grad, axis=0),
            jnp.dot(activated.T, seed_low, preferred_element_type=jnp.float32),
            bias_grad,
        )
        totals = (
            terms
            if totals is None
            else tuple((older + newer for older, newer in zip(totals, terms)))
        )
    totals = (
        lax.psum_scatter(
            totals[0].astype(jnp.bfloat16), "dp", scatter_dimension=0, tiled=True
        ).astype(jnp.float32),
        lax.psum_scatter(
            totals[1].astype(jnp.bfloat16), "dp", scatter_dimension=0, tiled=True
        ).astype(jnp.float32),
        lax.psum_scatter(
            totals[2].astype(jnp.bfloat16), "dp", scatter_dimension=0, tiled=True
        ).astype(jnp.float32),
        lax.psum_scatter(
            totals[3].astype(jnp.bfloat16), "dp", scatter_dimension=0, tiled=True
        ).astype(jnp.float32),
        lax.psum_scatter(
            totals[4].astype(jnp.bfloat16), "dp", scatter_dimension=0, tiled=True
        ).astype(jnp.float32),
        lax.psum_scatter(
            totals[5].astype(jnp.bfloat16), "dp", scatter_dimension=0, tiled=True
        ).astype(jnp.float32),
        lax.psum_scatter(
            totals[6].astype(jnp.bfloat16), "dp", scatter_dimension=1, tiled=True
        ).astype(jnp.float32),
        lax.psum_scatter(
            totals[7].astype(jnp.bfloat16), "dp", scatter_dimension=0, tiled=True
        ).astype(jnp.float32),
        lax.psum_scatter(
            totals[8].astype(jnp.bfloat16), "dp", scatter_dimension=0, tiled=True
        ).astype(jnp.float32),
        lax.psum_scatter(
            totals[9].astype(jnp.bfloat16), "dp", scatter_dimension=0, tiled=True
        ).astype(jnp.float32),
        lax.psum_scatter(
            totals[10].astype(jnp.bfloat16), "dp", scatter_dimension=1, tiled=True
        ).astype(jnp.float32),
        lax.psum_scatter(
            totals[11].astype(jnp.bfloat16), "dp", scatter_dimension=0, tiled=True
        ).astype(jnp.float32),
    )
    return (
        jnp.concatenate(outputs, axis=0),
        jnp.concatenate(back_rows, axis=0),
        totals[0],
        totals[1],
        totals[2],
        totals[3],
        totals[4],
        totals[5],
        totals[6],
        totals[7],
        totals[8],
        totals[9],
        totals[10],
        totals[11],
    )


def solution(mesh):
    placed = (
        P("dp", None),
        P("dp"),
        P("dp"),
        P("dp"),
        P("dp"),
        P("dp"),
        P("dp"),
        P("dp", "mp"),
        P(("mp", "dp")),
        P("mp", "dp"),
        P("dp"),
        P("dp", "mp"),
        P(("mp", "dp")),
        P("mp", "dp"),
        P("dp"),
        P("dp", None),
    )
    return jax.shard_map(
        shards,
        mesh=mesh,
        in_specs=placed,
        out_specs=(
            P("dp", None),
            P("dp", None),
            P("dp"),
            P("dp"),
            P("dp"),
            P("dp"),
            P("dp", "mp"),
            P(("mp", "dp")),
            P("mp", "dp"),
            P("dp"),
            P("dp", "mp"),
            P(("mp", "dp")),
            P("mp", "dp"),
            P("dp"),
        ),
        check_vma=False,
    )
```

profile of v0, /device:TPU:0, one launch (start us, length us, event | category | flops | bytes accessed | tf_op | source)
XLA Modules:
  0.0 900.6 jit_solution(295608793468583112)
XLA Ops:
  16.2 15.3 %all-reduce = bf16[1536]{0:T(1024)(128)(2,1)S(1)} all-reduce(bf16[1536]{0:T(1024)(128)(2,1)S(1)} %dynamic-update-slice), channel_id=1, replica_groups=mesh['dp'=8,'mp'=4] {'dp'}, use_global_device_ids=true, to_apply=%add | all-reduce | flops 1536 | bytes 6144
  32.7 8.3 all-gather.4
  41.0 8.9 all-gather.3
  49.9 8.2 all-gather.2
  58.0 8.9 all-gather.1
  66.9 8.3 all-gather
  90.5 8.6 convolution_add_fusion
  120.9 5.1 convolution_add_fusion.1
  166.7 9.3 %fusion.94 = f32[2048,1536]{1,0:T(8,128)} fusion(bf16[512,1536]{0,1:T(8,128)(2,1)S(1)} %bitcast.127, f32[2048]{0:T(1024)S(1)} %bitcast.161, f32[2048]{0:T(1024)S(1)} %bitcast.142, f32[512]{0:T(512)S(1)} %add_rsqrt_fusion.1, f32[512]{0:T(512)S(1)} %broadcast_multiply_fusion.5, bf16[1024,2048]{1,0:T(8,128)(2,1)} %param.16), kind=kOutput, calls=%fused_computation.213 | convolution fusion | flops 3227516928 | bytes 16273408 | tf_op jit(solution)/shard_map/dot_general | solution.py:315
  176.0 8.9 add_convert_fusion.2
  185.0 7.5 convolution_convert_fusion.1
  192.5 7.9 convolution_convert_fusion.3
  200.4 10.6 %fusion.98 = f32[512,2048]{1,0:T(8,128)} fusion(bf16[2048,2048]{1,0:T(8,128)(2,1)} %all-gather.16.cloned.1.call-done, f32[512]{0:T(512)S(1)} %add_rsqrt_fusion, f32[512]{0:T(512)S(1)} %broadcast_multiply_fusion.4, f32[2048]{0:T(1024)S(1)} %bitcast.149, f32[2048]{0:T(1024)S(1)} %bitcast.133, bf16[1024,2048]{1,0:T(8,128)(2,1)} %param.16), kind=kOutput, calls=%fused_computation.214 | convolution fusion | flops 4301258752 | bytes 14700544 | tf_op jit(solution)/shard_map/dot_general | solution.py:231
  211.0 10.0 %fusion.112 = f32[512,2048]{1,0:T(8,128)S(1)} fusion(bf16[2048,2048]{1,0:T(8,128)(2,1)} %all-gather.18.cloned.1.call-done, f32[512,2048]{1,0:T(8,128)} %fusion.98, f32[2048]{0:T(1024)S(1)} %bitcast.153), kind=kOutput, calls=%fused_computation.217 | convolution fusion | flops 4301258752 | bytes 16785408 | tf_op jit(solution)/shard_map/dot_general | solution.py:237
  223.8 4.6 fusion.92
  230.4 4.7 fusion.113
  237.9 8.8 fusion.119
  246.7 7.7 convolution_convert_fusion
  254.3 9.0 fusion.118
  263.3 7.9 convolution_convert_fusion.2
  271.3 14.3 %fusion.102 = f32[2048,2048]{1,0:T(8,128)} fusion(f32[512]{0:T(512)S(1)} %get-tuple-element.188, bf16[1024,2048]{1,0:T(8,128)(2,1)} %param.31, f32[512,2048]{1,0:T(8,128)} %copy-done.64, f32[2048]{0:T(1024)S(1)} %bitcast.157), kind=kOutput, calls=%fused_computation.215 | convolution fusion | flops 4304404480 | bytes 23078912 | tf_op jit(solution)/shard_map/dot_general | solution.py:321
  285.6 10.5 %add_convert_fusion = bf16[2048,2048]{1,0:T(8,128)(2,1)} fusion(f32[2048,2048]{1,0:T(8,128)} %fusion.102, f32[512]{0:T(512)S(1)} %get-tuple-element.189, bf16[1024,2048]{1,0:T(8,128)(2,1)S(1)} %copy-done.9, f32[512,2048]{1,0:T(8,128)S(1)} %copy-done.65, f32[2048]{0:T(1024)S(1)} %bitcast.158), kind=kOutput, calls=%fused_computation | convolution fusion | flops 4312793088 | bytes 31467520 | tf_op jit(solution)/shard_map/dot_general | solution.py:321
  297.7 10.6 %fusion.72 = f32[2048,2048]{1,0:T(8,128)} fusion(bf16[512,2048]{1,0:T(8,128)(2,1)S(1)} %copy-done.66, f32[2048]{0:T(1024)S(1)} %bitcast.151, f32[2048]{0:T(1024)S(1)} %bitcast.135, f32[512]{0:T(512)S(1)} %add_rsqrt_fusion.1, f32[512]{0:T(512)S(1)} %broadcast_multiply_fusion.5, bf16[1024,2048]{1,0:T(8,128)(2,1)} %param.16), kind=kOutput, calls=%fused_computation.147 | convolution fusion | flops 4301258752 | bytes 20992000 | tf_op jit(solution)/shard_map/dot_general | solution.py:319
  308.3 11.3 %add_convert_fusion.1 = bf16[2048,2048]{1,0:T(8,128)(2,1)} fusion(f32[2048,2048]{1,0:T(8,128)} %fusion.72, bf16[512,2048]{1,0:T(8,128)(2,1)} %get-tuple-element.211, f32[512]{0:T(512)S(1)} %add_rsqrt_fusion, f32[512]{0:T(512)S(1)} %broadcast_multiply_fusion.4, f32[2048]{0:T(1024)S(1)} %bitcast.152, f32[2048]{0:T(1024)S(1)} %bitcast.136, ...), kind=kOutput, calls=%fused_computation.1 | convolution fusion | flops 4309647360 | bytes 29380608 | tf_op jit(solution)/shard_map/dot_general | solution.py:319
  322.2 8.7 all-gather.6
  330.9 8.2 all-gather.5
  345.7 395.6 %all-reduce.12.cloned.1.call-done = (bf16[512,2048]{1,0:T(8,128)(2,1)}, bf16[512,2048]{1,0:T(8,128)(2,1)}, bf16[512,2048]{1,0:T(8,128)(2,1)}, bf16[512,2048]{1,0...) async-done(((bf16[512,2048]{1,0:T(8,128)(2,1)}, bf16[512,2048]{1,0:T(8,128)(2,1)}, bf16[512,2048]{1,0:T(8,128)(2,1)}, bf16[512,2048]{1,0:T(8,128)(2,1)}, ...) | async-done | bytes 12582928 | tf_op jit(solution)/shard_map/psum | solution.py:238
  741.4 9.7 %fusion.45 = (f32[2048]{0:T(1024)S(1)}, f32[512]{0:T(512)S(1)}, f32[2048]{0:T(1024)S(1)}, f32[2048]{0:T(1024)S(1)}, f32[512]{0:T(512)S(1)}, /*index=5*/f32[2048]...) fusion(bf16[512,2048]{1,0:T(8,128)(2,1)} %get-tuple-element.154, ...), kind=kLoop, calls=%fused_computation.68 | loop fusion | flops 35633152 | bytes 12681216 | tf_op jit(solution)/shard_map/reduce_sum | solution.py:313
  755.5 25.6 %all-reduce.8 = (bf16[2048]{0:T(1024)(128)(2,1)S(1)}, bf16[2048]{0:T(1024)(128)(2,1)S(1)}, bf16[2048]{0:T(1024)(128)(2,1)S(1)}, bf16[2048]{0:T(1024)(128)(2,1)S(...) all-reduce(bf16[2048]{0:T(1024)(128)(2,1)S(1)} %add_convert_fusion., ...), channel_id=2, replica_groups=mesh['dp'=8,'mp'=4] {'dp'}, use_global_device_ids=true, to_apply=%region_24.25.clone | all-reduce | flops 13824 | bytes 55296
  781.2 34.1 %reduce-scatter.11.cloned.1.call-done = bf16[2048,256]{1,0:T(8,128)(2,1)} async-done(((bf16[2048,2048]{1,0:T(8,128)(2,1)}), bf16[2048,256]{1,0:T(8,128)(2,1)}) %reduce-scatter.11.cloned.1.call-update) | async-done | bytes 1048592 | tf_op jit(solution)/shard_map/reduce_scatter | solution.py:360
  821.7 8.1 fusion.34
  835.4 54.8 %reduce-scatter.9.cloned.1.call-done = bf16[256,2048]{1,0:T(8,128)(2,1)} async-done(((bf16[2048,2048]{1,0:T(8,128)(2,1)}), bf16[256,2048]{1,0:T(8,128)(2,1)}) %reduce-scatter.9.cloned.1.call-update) | async-done | bytes 1048592 | tf_op jit(solution)/shard_map/reduce_scatter | solution.py:354
  (282 shorter events, 122.1 us)
Async XLA Ops:
  7.2 76.6 %all-gather.14.cloned.1.call-start = ((), (), s32[]{:S(2)}) async-start(), calls=%async_computation.5 | async-start | bytes 2359296 | tf_op jit(solution)/shard_map/all_gather | solution.py:185
  7.9 82.6 %all-gather.12.cloned.1.call-start = ((), (), s32[]{:S(2)}) async-start(), calls=%async_computation.4 | async-start | bytes 7077888 | tf_op jit(solution)/shard_map/all_gather | solution.py:183
  8.7 191.8 %all-gather.16.cloned.1.call-start = ((), (), s32[]{:S(2)}) async-start(), calls=%async_computation.6 | async-start | bytes 9437184 | tf_op jit(solution)/shard_map/all_gather | solution.py:187
  9.4 201.6 %all-gather.18.cloned.1.call-start = ((), (), s32[]{:S(2)}) async-start(), calls=%async_computation.7 | async-start | bytes 9437184 | tf_op jit(solution)/shard_map/all_gather | solution.py:189
  10.0 331.5 %reduce-scatter.7.cloned.1.call-start = ((), (), s32[]{:S(2)}) async-start(), calls=%async_computation.9 | async-start | bytes 2359296 | tf_op jit(solution)/shard_map/reduce_scatter | solution.py:348
  31.5 46.6 %copy-start = (bf16[1024,2048]{1,0:T(8,128)(2,1)S(1)}, bf16[1024,2048]{1,0:T(8,128)(2,1)}, u32[]{:S(2)}) copy-start(bf16[1024,2048]{1,0:T(8,128)(2,1)} %param.16) | copy-start | bytes 12582916
  75.2 100.7 %copy-start.57 = (f32[8,1,256]{2,1,0:T(1,128)}, f32[8,1,256]{2,1,0:T(1,128)S(1)}, u32[]{:S(2)}) copy-start(f32[8,1,256]{2,1,0:T(1,128)S(1)} %convert_element_type.396) | copy-start | bytes 24580
  112.6 8.0 slice-start.2
  142.7 12.4 %copy-start.11 = (f32[512,2,1,256]{3,0,1,2:T(8,128)}, f32[512,2,1,256]{3,0,1,2:T(8,128)S(1)}, u32[]{:S(2)}) copy-start(f32[512,2,1,256]{3,0,1,2:T(8,128)S(1)} %convolution_bitcast_fusion.2) | copy-start | bytes 3145732
  150.5 192.7 %reduce-scatter.5.cloned.1.call-start = ((), (), s32[]{:S(2)}) async-start(), calls=%async_computation.8 | async-start | bytes 7077888 | tf_op jit(solution)/shard_map/reduce_scatter | solution.py:342
  166.7 9.3 %copy-start.2 = (bf16[1024,2048]{1,0:T(8,128)(2,1)S(1)}, bf16[1024,2048]{1,0:T(8,128)(2,1)}, u32[]{:S(2)}) copy-start(bf16[1024,2048]{1,0:T(8,128)(2,1)} %param.16) | copy-start | bytes 12582916
  166.7 9.3 %copy-start.52 = (bf16[512,2,3,256]{0,3,2,1:T(8,128)(2,1)S(1)}, bf16[512,2,3,256]{0,3,2,1:T(8,128)(2,1)}, u32[]{:S(2)}) copy-start(bf16[512,2,3,256]{0,3,2,1:T(8,128)(2,1)} %copy.127) | copy-start | bytes 4718596
  184.9 556.4 %all-reduce.12.cloned.1.call-start = ((), (), s32[]{:S(2)}) async-start(), calls=%async_computation.12 | async-start | bytes 25165824 | tf_op jit(solution)/shard_map/psum | solution.py:238
  211.0 10.0 %copy-start.35 = (bf16[512,2048]{1,0:T(8,128)(2,1)S(1)}, bf16[512,2048]{1,0:T(8,128)(2,1)}, u32[]{:S(2)}) copy-start(bf16[512,2048]{1,0:T(8,128)(2,1)} %all-gather.14.cloned.1.call-done) | copy-start | bytes 6291460
  211.0 10.0 %copy-start.39 = (bf16[2,256,512]{2,1,0:T(8,128)(2,1)S(1)}, bf16[2,256,512]{2,1,0:T(8,128)(2,1)}, u32[]{:S(2)}) copy-start(bf16[2,256,512]{2,1,0:T(8,128)(2,1)} %get-tuple-element.205) | copy-start | bytes 1572868
  211.0 12.7 %copy-start.61 = (bf16[2048,2048]{1,0:T(8,128)(2,1)S(1)}, bf16[2048,2048]{1,0:T(8,128)(2,1)}, u32[]{:S(2)}) copy-start(bf16[2048,2048]{1,0:T(8,128)(2,1)} %all-gather.16.cloned.1.call-done) | copy-start | bytes 25165828
  221.1 9.4 %slice-start = ((s8[8388608]{0:T(1024)(128)(4,1)}), s8[4194304]{0:T(1024)(128)(4,1)S(1)}, s32[]{:S(2)}) async-start(s8[8388608]{0:T(1024)(128)(4,1)} %bitcast.163), calls=%async_computation.13 | async-start | bytes 8388608
  271.2 544.0 %reduce-scatter.11.cloned.1.call-start = ((), (), s32[]{:S(2)}) async-start(), calls=%async_computation.11 | async-start | bytes 9437184 | tf_op jit(solution)/shard_map/reduce_scatter | solution.py:360
  271.3 14.3 %copy-start.9 = (bf16[1024,2048]{1,0:T(8,128)(2,1)S(1)}, bf16[1024,2048]{1,0:T(8,128)(2,1)}, u32[]{:S(2)}) copy-start(bf16[1024,2048]{1,0:T(8,128)(2,1)} %param.31) | copy-start | bytes 12582916
  271.3 14.3 %copy-start.65 = (f32[512,2048]{1,0:T(8,128)S(1)}, f32[512,2048]{1,0:T(8,128)}, u32[]{:S(2)}) copy-start(f32[512,2048]{1,0:T(8,128)} %fusion.98) | copy-start | bytes 12582916
  296.1 594.1 %reduce-scatter.9.cloned.1.call-start = ((), (), s32[]{:S(2)}) async-start(), calls=%async_computation.10 | async-start | bytes 9437184 | tf_op jit(solution)/shard_map/reduce_scatter | solution.py:354
  297.7 10.6 %copy-start.4 = (bf16[1024,2048]{1,0:T(8,128)(2,1)S(1)}, bf16[1024,2048]{1,0:T(8,128)(2,1)}, u32[]{:S(2)}) copy-start(bf16[1024,2048]{1,0:T(8,128)(2,1)} %param.16) | copy-start | bytes 12582916
  319.6 19.5 %copy-start.12 = (f32[512,2,1,256]{3,0,1,2:T(8,128)S(1)}, f32[512,2,1,256]{3,0,1,2:T(8,128)}, u32[]{:S(2)}) copy-start(f32[512,2,1,256]{3,0,1,2:T(8,128)} %copy-done.11) | copy-start | bytes 3145732
  319.6 19.5 %copy-start.14 = (f32[512,2,1,256]{3,0,1,2:T(8,128)S(1)}, f32[512,2,1,256]{3,0,1,2:T(8,128)}, u32[]{:S(2)}) copy-start(f32[512,2,1,256]{3,0,1,2:T(8,128)} %copy-done.13) | copy-start | bytes 3145732
  319.6 19.5 %copy-start.16 = (f32[512,2,1,256]{3,0,1,2:T(8,128)S(1)}, f32[512,2,1,256]{3,0,1,2:T(8,128)}, u32[]{:S(2)}) copy-start(f32[512,2,1,256]{3,0,1,2:T(8,128)} %copy-done.15) | copy-start | bytes 3145732
  339.1 402.2 %copy-start.58 = (f32[8,1,256]{2,1,0:T(1,128)S(1)}, f32[8,1,256]{2,1,0:T(1,128)}, u32[]{:S(2)}) copy-start(f32[8,1,256]{2,1,0:T(1,128)} %copy-done.57) | copy-start | bytes 24580
  741.4 9.7 %copy-start.5 = (bf16[1024,2048]{1,0:T(8,128)(2,1)S(1)}, bf16[1024,2048]{1,0:T(8,128)(2,1)}, u32[]{:S(2)}) copy-start(bf16[1024,2048]{1,0:T(8,128)(2,1)} %param.16) | copy-start | bytes 12582916
  741.4 9.8 %copy-start.10 = (bf16[1024,2048]{1,0:T(8,128)(2,1)S(1)}, bf16[1024,2048]{1,0:T(8,128)(2,1)}, u32[]{:S(2)}) copy-start(bf16[1024,2048]{1,0:T(8,128)(2,1)} %param.31) | copy-start | bytes 12582916
  741.4 9.8 %copy-start.27 = (bf16[512,2048]{1,0:T(8,128)(2,1)S(1)}, bf16[512,2048]{1,0:T(8,128)(2,1)}, u32[]{:S(2)}) copy-start(bf16[512,2048]{1,0:T(8,128)(2,1)} %get-tuple-element.154) | copy-start | bytes 6291460
  741.4 9.8 %copy-start.28 = (bf16[512,2048]{1,0:T(8,128)(2,1)S(1)}, bf16[512,2048]{1,0:T(8,128)(2,1)}, u32[]{:S(2)}) copy-start(bf16[512,2048]{1,0:T(8,128)(2,1)} %get-tuple-element.155) | copy-start | bytes 6291460
  755.5 66.3 %copy-start.26 = (bf16[512,2048]{1,0:T(8,128)(2,1)S(1)}, bf16[512,2048]{1,0:T(8,128)(2,1)}, u32[]{:S(2)}) copy-start(bf16[512,2048]{1,0:T(8,128)(2,1)} %get-tuple-element.152) | copy-start | bytes 6291460
  781.1 111.8 %copy-start.60 = (f32[256]{0:T(256)}, f32[256]{0:T(256)S(1)}, u32[]{:S(2)}) copy-start(f32[256]{0:T(256)S(1)} %dynamic-slice_convert_fusion.1) | copy-start | bytes 3076
  (48 other events, 135.5 us)
Sparse Core Ops, SparseCore 0:
  9.9 30.8 all-gather.13
  42.7 45.4 all-gather.11
  90.0 54.2 all-gather.15
  146.1 55.8 all-gather.17
  205.1 41.1 reduce-scatter.6
  249.5 61.7 reduce-scatter.4
  315.1 426.1 all-reduce.11
  744.8 70.3 reduce-scatter.10
  818.7 71.4 reduce-scatter.8
where the time goes:
time: 908 us; the launch traced here: 901 us
  waiting for transfers between devices  487 us (54%)
  matrix products  184 us (20%)
  blocking collectives  100 us (11%)
  other arithmetic  66.2 us (7%)
  local copies, waits for them, and re-layouts  44.1 us (5%)
  between operations  18.6 us (2%)
    psum x1, waiting for transfers between devices, shards(): lax.psum(branch_part.astype(jnp.bfloat16), 'mp').astype(jnp.float32)  396 us
    reduce_scatter x1, waiting for transfers between devices, shards(): lax.psum_scatter(totals[8].astype(jnp.bfloat16), 'dp', scatter_dimension=...  54.8 us
    unnamed x2, blocking collectives  40.9 us
    reduce_scatter x1, waiting for transfers between devices, shards(): lax.psum_scatter(totals[10].astype(jnp.bfloat16), 'dp', scatter_dimension...  34.1 us
    dot_general x2, matrix products, shards(): jnp.dot(activated.T, seed_low, preferred_element_type=jnp.float32)  24.8 us
    dot_general x2, matrix products, shards(): jnp.dot(hidden_two.T, before_low, preferred_element_type=jnp.float32)  21.9 us
    unnamed x157, local copies, waits for them, and re-layouts  21.2 us
    dot_general x2, matrix products, shards(): jnp.dot(hidden_one.T, joint_low, preferred_element_type=jnp.float32)  18.2 us
  transfers between devices with their start and end apart: 9, of which 3 were waited for; matrix products, arithmetic and copies ran while one was open for 31% of the time, Pallas kernels for 0%

commit v1 on v0

v1 whole, which is shorter than its diff:
```python
import math

import jax
import jax.numpy as jnp
from jax import lax
from jax.experimental import pallas as pl
from jax.experimental.pallas import tpu as pltpu
from jax.sharding import PartitionSpec as P

HD = 256
ROT = 64
BLOCK = 512
LANES = 128
PIECES = 8

EPS = 1e-05
NEGATIVE = -1e30
ROOT_HALF = 0.7071067811865476
ROOT_TWOPI = 2.5066282746310002
F32 = jnp.float32
BF16 = jnp.bfloat16


def nt(a, b):
    return lax.dot_general(a, b, (((1,), (1,)), ((), ())), preferred_element_type=F32)


def tn(a, b):
    return lax.dot_general(a, b, (((0,), (0,)), ((), ())), preferred_element_type=F32)


def nn(a, b):
    return lax.dot_general(a, b, (((1,), (0,)), ((), ())), preferred_element_type=F32)


def call(kernel, out_shape, flops, nbytes, extra=0, **more):
    return pl.pallas_call(
        kernel,
        out_shape=out_shape,
        compiler_params=pltpu.CompilerParams(vmem_limit_bytes=56 << 20),
        cost_estimate=pl.CostEstimate(
            flops=flops, bytes_accessed=nbytes, transcendentals=extra
        ),
        **more,
    )


def shape(*dims, dtype=BF16):
    return jax.ShapeDtypeStruct(dims, dtype)


def whole(*dims):
    return pl.BlockSpec(dims, lambda *_: (0,) * len(dims))


def folded(values):
    return jnp.sum(values.reshape(-1, 8, values.shape[1]), axis=0)


def accumulate(ref, at, values, first):
    @pl.when(first)
    def _():
        ref[:, at] = values

    @pl.when(jnp.logical_not(first))
    def _():
        ref[:, at] += values


def rows_kernel(
    where_ref, in_ref, cot_ref, pad_ref, vec_ref, one_ref, two_ref, norm_ref, seed_ref, sum_ref
):
    x = in_ref[...].astype(F32)
    mean = jnp.mean(x, axis=1, keepdims=True)
    centred = x - mean
    inv = lax.rsqrt(jnp.mean(centred * centred, axis=1, keepdims=True) + EPS)
    marks = pad_ref[...].astype(F32)
    width = x.shape[1] // PIECES
    first = pl.program_id(0) == 0
    for r in range(PIECES):
        source = pl.ds(pl.multiple_of(where_ref[r] * width, width), width)
        at = slice(r * width, (r + 1) * width)
        normed = (in_ref[:, source].astype(F32) - mean) * inv
        norm_ref[:, at] = normed.astype(BF16)
        one_ref[:, at] = (normed * vec_ref[0:1, at] + vec_ref[1:2, at]).astype(BF16)
        two_ref[:, at] = (normed * vec_ref[2:3, at] + vec_ref[3:4, at]).astype(BF16)
        seed = cot_ref[:, source].astype(F32) * marks
        seed_ref[:, at] = seed.astype(BF16)
        accumulate(sum_ref, at, folded(seed), first)


def rows_pass(where, inputs, cotangent, marks, vectors):
    total, features = inputs.shape
    tile = total // 8
    wide = pl.BlockSpec((tile, features), lambda i, w: (i, 0))
    return call(
        rows_kernel,
        [shape(total, features)] * 4 + [shape(8, features, dtype=F32)],
        40 * total * features,
        12 * total * features,
        grid_spec=pltpu.PrefetchScalarGridSpec(
            num_scalar_prefetch=1,
            grid=(8,),
            in_specs=[
                wide,
                wide,
                pl.BlockSpec((tile, 1), lambda i, w: (i, 0)),
                whole(vectors.shape[0], features),
            ],
            out_specs=[wide] * 4 + [whole(8, features)],
        ),
    )(where, inputs, cotangent, marks, vectors)


def joint_kernel(*refs):
    lhs, pieces, bias, out = refs[0], refs[1 : 1 + PIECES], refs[-2], refs[-1]
    weight = jnp.concatenate([p[...] for p in pieces], axis=0)
    out[...] = nn(lhs[...], weight) + bias[...]


def project(hidden, pieces, bias):
    total, features = hidden.shape
    depth, width = pieces[0].shape
    tile = 512
    return call(
        joint_kernel,
        shape(total, width, dtype=F32),
        2 * total * features * width,
        2 * features * (total + width) + 4 * total * width,
        grid=(width // tile,),
        in_specs=[whole(total, features)]
        + [pl.BlockSpec((depth, tile), lambda n: (0, n))] * PIECES
        + [pl.BlockSpec((1, tile), lambda n: (0, n))],
        out_specs=pl.BlockSpec((total, tile), lambda n: (0, n)),
    )(hidden, *pieces, bias)


def expand_kernel(*refs):
    lhs, pieces, bias, act, slope = refs[0], refs[1 : 1 + PIECES], refs[-3], refs[-2], refs[-1]
    weight = jnp.concatenate([p[...] for p in pieces], axis=0)
    u = nn(lhs[...], weight) + bias[...]
    phi = 0.5 * (1.0 + lax.erf(u * ROOT_HALF))
    act[...] = (u * phi).astype(BF16)
    slope[...] = (phi + u * jnp.exp(-0.5 * u * u) * (1.0 / ROOT_TWOPI)).astype(BF16)


def expand(hidden, pieces, bias):
    total, features = hidden.shape
    depth, width = pieces[0].shape
    tile = 256
    return call(
        expand_kernel,
        [shape(total, width)] * 2,
        2 * total * features * width,
        2 * features * (total + width) + 4 * total * width,
        2 * total * width,
        grid=(width // tile,),
        in_specs=[whole(total, features)]
        + [pl.BlockSpec((depth, tile), lambda n: (0, n))] * PIECES
        + [pl.BlockSpec((1, tile), lambda n: (0, n))],
        out_specs=[pl.BlockSpec((total, tile), lambda n: (0, n))] * 2,
    )(hidden, *pieces, bias)


def mixture_kernel(*refs):
    lhs, pieces, out = refs[0], refs[1 : 1 + PIECES], refs[-1]
    weight = jnp.concatenate([p[...] for p in pieces], axis=1)
    out[...] = nt(lhs[...], weight).astype(BF16)


def mixture_back(seed, pieces):
    total, features = seed.shape
    width, depth = pieces[0].shape
    tile = 256
    return call(
        mixture_kernel,
        shape(total, width),
        2 * total * features * width,
        2 * features * (total + width) + 2 * total * width,
        grid=(width // tile,),
        in_specs=[whole(total, features)]
        + [pl.BlockSpec((tile, depth), lambda n: (n, 0))] * PIECES,
        out_specs=pl.BlockSpec((total, tile), lambda n: (0, n)),
    )(seed, *pieces)


def before_kernel(*refs):
    lhs, pieces, slope, low, sums = refs[0], refs[1 : 1 + PIECES], refs[-3], refs[-2], refs[-1]
    weight = jnp.concatenate([p[...] for p in pieces], axis=1)
    grad = nt(lhs[...], weight) * slope[...].astype(F32)
    low[...] = grad.astype(BF16)
    sums[...] = folded(grad)


def before_back(seed, pieces, slope):
    total, features = seed.shape
    width, depth = pieces[0].shape
    tile = 512
    return call(
        before_kernel,
        [shape(total, width), shape(8, width, dtype=F32)],
        2 * total * features * width,
        2 * features * (total + width) + 4 * total * width,
        grid=(width // tile,),
        in_specs=[whole(total, features)]
        + [pl.BlockSpec((tile, depth), lambda n: (n, 0))] * PIECES
        + [pl.BlockSpec((total, tile), lambda n: (0, n))],
        out_specs=[
            pl.BlockSpec((total, tile), lambda n: (0, n)),
            pl.BlockSpec((8, tile), lambda n: (0, n)),
        ],
    )(seed, *pieces, slope)


def loads(pieces, scratch, sems):
    copies = []
    for r, p in enumerate(pieces):
        axis = 0 if scratch.shape[1] == 2 * p.shape[0] else 1
        side = pl.ds((r % 2) * p.shape[axis], p.shape[axis])
        slot = scratch.at[r // 2, side] if axis == 0 else scratch.at[r // 2, :, side]
        copies.append(pltpu.make_async_copy(p, slot, sems.at[r // 2]))
    return copies


def arrived(groups, at):
    @pl.when(at == 0)
    def _():
        for copies in zip(*(loads(*group) for group in groups)):
            for copy in copies:
                copy.start()

    for pieces, scratch, sems in groups:
        slot = scratch.at[at]
        pltpu.make_async_copy(slot, slot, sems.at[at]).wait()


def held(pieces, axis):
    rows, columns = pieces[0].shape
    slot = (2 * rows, columns) if axis == 0 else (rows, 2 * columns)
    return [
        pltpu.VMEM((PIECES // 2,) + slot, BF16),
        pltpu.SemaphoreType.DMA((PIECES // 2,)),
    ]


def branch_kernel(*refs):
    mix, act = refs[0], refs[1]
    dense, reduce = refs[2 : 2 + PIECES], refs[2 + PIECES : 2 + 2 * PIECES]
    out, dense_vm, dense_sem, reduce_vm, reduce_sem = refs[-5:]
    r = pl.program_id(0)
    arrived(((dense, dense_vm, dense_sem), (reduce, reduce_vm, reduce_sem)), r)
    out[...] = (nn(mix[...], dense_vm[r]) + nn(act[...], reduce_vm[r])).astype(BF16)


def branch_of(mixture, activated, dense, reduce):
    total = mixture.shape[0]
    width = dense[0].shape[1]
    depth = mixture.shape[1] + activated.shape[1]
    return call(
        branch_kernel,
        shape(total, PIECES * width),
        2 * total * depth * PIECES * width,
        2 * depth * (total + PIECES * width) + 2 * total * PIECES * width,
        grid=(PIECES // 2,),
        in_specs=[whole(*mixture.shape), whole(*activated.shape)]
        + [pl.BlockSpec(memory_space=pl.ANY)] * (2 * PIECES),
        out_specs=pl.BlockSpec((total, 2 * width), lambda r: (0, r)),
        scratch_shapes=held(dense, 1) + held(reduce, 1),
    )(mixture, activated, *dense, *reduce)


def gx_kernel(*refs):
    low_one, low_two, norm, vec = refs[:4]
    joint, wide = refs[4 : 4 + PIECES], refs[4 + PIECES : 4 + 2 * PIECES]
    out, gains, joint_vm, joint_sem, wide_vm, wide_sem = refs[-6:]
    r = pl.program_id(0)
    arrived(((joint, joint_vm, joint_sem), (wide, wide_vm, wide_sem)), r)
    one = nt(low_one[...], joint_vm[r])
    two = nt(low_two[...], wide_vm[r])
    out[...] = (one * vec[0:1, :] + two * vec[2:3, :]).astype(BF16)
    normed = norm[...].astype(F32)
    gains[0:8, :] = folded(one * normed)
    gains[8:16, :] = folded(one)
    gains[16:24, :] = folded(two * normed)
    gains[24:32, :] = folded(two)


def gx_of(joint_low, before_low, normed, vectors, joint, wide):
    total, features = normed.shape
    depth = joint_low.shape[1] + before_low.shape[1]
    each = 2 * features // PIECES
    return call(
        gx_kernel,
        [shape(total, features), shape(32, features, dtype=F32)],
        2 * total * depth * features,
        2 * depth * (total + features) + 4 * total * features,
        grid=(PIECES // 2,),
        in_specs=[
            whole(*joint_low.shape),
            whole(*before_low.shape),
            pl.BlockSpec((total, each), lambda r: (0, r)),
            pl.BlockSpec((vectors.shape[0], each), lambda r: (0, r)),
        ]
        + [pl.BlockSpec(memory_space=pl.ANY)] * (2 * PIECES),
        out_specs=[
            pl.BlockSpec((total, each), lambda r: (0, r)),
            pl.BlockSpec((32, each), lambda r: (0, r)),
        ],
        scratch_shapes=held(joint, 0) + held(wide, 0),
    )(joint_low, before_low, normed, vectors, *joint, *wide)


def gradient_kernel(where_ref, *refs):
    sides = len(refs) // 2
    lhs, rhs, out = refs[:sides], refs[sides : 2 * sides], refs[-1]
    start = 0
    for left, right in zip(lhs, rhs):
        stop = start + right.shape[1]
        out[:, start:stop] = tn(left[...], right[...]).astype(BF16)
        start = stop


def gradient(where, lhs, rhs):
    total, features = lhs[0].shape
    width = sum(a.shape[1] for a in rhs)
    each = features // PIECES
    return call(
        gradient_kernel,
        shape(features, width),
        2 * total * features * width,
        2 * len(lhs) * total * features + 2 * total * width + 2 * features * width,
        grid_spec=pltpu.PrefetchScalarGridSpec(
            num_scalar_prefetch=1,
            grid=(PIECES,),
            in_specs=[pl.BlockSpec((total, each), lambda r, w: (0, r))] * len(lhs)
            + [whole(*a.shape) for a in rhs],
            out_specs=pl.BlockSpec((each, width), lambda r, w: (w[r], 0)),
        ),
    )(where, *lhs, *rhs)


def rotary_tables(segments):
    rows = segments.reshape(-1, BLOCK)
    indices = jnp.arange(BLOCK)
    matching = rows[:, :, None] == rows[:, None, :]
    earlier = indices[None, :] < indices[:, None]
    positions = jnp.sum((matching & earlier[None]).astype(jnp.int32), axis=2)
    positions = positions.astype(F32).reshape(-1)
    half = ROT // 2
    frequency = jnp.exp(jnp.arange(half, dtype=F32) * (-2.0 * math.log(10000.0) / ROT))
    angles = positions[:, None] * frequency[None, :]
    cosine, sine = jnp.cos(angles), jnp.sin(angles)
    pad = jnp.ones((angles.shape[0], LANES - ROT), F32)
    return (
        jnp.concatenate([cosine, cosine, pad], axis=1),
        jnp.concatenate([-sine, sine, 0.0 * pad], axis=1),
    )


def swap_halves(first):
    lane = lax.broadcasted_iota(jnp.int32, first.shape, 1)
    return jnp.where(
        lane < ROT // 2,
        pltpu.roll(first, LANES - ROT // 2, 1),
        pltpu.roll(first, ROT // 2, 1),
    )


def attend_kernel(
    joint_ref, grad_ref, cos_ref, sin_ref, col_ref, row_ref, mix_ref, low_ref, bias_ref
):
    cosine, sine = cos_ref[...], sin_ref[...]

    def rotate(t):
        first = t[:, :LANES]
        return jnp.concatenate(
            [first * cosine + swap_halves(first) * sine, t[:, LANES:]], axis=1
        )

    def unrotate(t):
        first = t[:, :LANES]
        return jnp.concatenate(
            [first * cosine - swap_halves(first) * sine, t[:, LANES:]], axis=1
        )

    scale = HD ** (-0.5)
    queries = (rotate(joint_ref[:, :HD]) * scale).astype(BF16)
    keys = rotate(joint_ref[:, HD : 2 * HD]).astype(BF16)
    values = joint_ref[:, 2 * HD :].astype(BF16)
    grad = grad_ref[...]
    scores = nt(queries, keys)
    size = scores.shape
    allowed = (col_ref[...] == row_ref[0]) & (
        lax.broadcasted_iota(jnp.int32, size, 1) <= lax.broadcasted_iota(jnp.int32, size, 0)
    )
    scores = jnp.where(allowed, scores, NEGATIVE)
    peak = jnp.max(scores, axis=1, keepdims=True)
    chances = jnp.exp(scores - peak)
    chances = chances * (1.0 / jnp.sum(chances, axis=1, keepdims=True))
    weights = chances.astype(BF16)
    mixture = nn(weights, values).astype(BF16)
    mix_ref[...] = mixture
    value_grad = tn(weights, grad)
    weight_grad = nt(grad, values)
    delta = jnp.sum(grad.astype(F32) * mixture.astype(F32), axis=1, keepdims=True)
    score_grad = (chances * (weight_grad - delta)).astype(BF16)
    query_grad = unrotate(nn(score_grad, keys)) * scale
    key_grad = unrotate(tn(score_grad, queries))
    first = pl.program_id(1) == 0
    for at, piece in enumerate((query_grad, key_grad, value_grad)):
        at = slice(at * HD, (at + 1) * HD)
        low_ref[:, at] = piece.astype(BF16)
        accumulate(bias_ref, at, folded(piece), first)


def attend(joint, grad_mixture, cosine, sine, column, segments):
    total, width = joint.shape
    heads, blocks = width // (3 * HD), total // BLOCK
    table = pl.BlockSpec((BLOCK, LANES), lambda h, b: (b, 0))
    wide = pl.BlockSpec((BLOCK, 3 * HD), lambda h, b: (b, h))
    narrow = pl.BlockSpec((BLOCK, HD), lambda h, b: (b, h))
    return call(
        attend_kernel,
        [shape(total, heads * HD), shape(total, width), shape(8, width, dtype=F32)],
        14 * total * BLOCK * heads * HD,
        total * width * 8,
        total * BLOCK * heads,
        grid=(heads, blocks),
        in_specs=[
            wide,
            narrow,
            table,
            table,
            pl.BlockSpec((BLOCK, 1), lambda h, b: (b, 0)),
            pl.BlockSpec((1, 1, BLOCK), lambda h, b: (b, 0, 0)),
        ],
        out_specs=[narrow, wide, pl.BlockSpec((8, 3 * HD), lambda h, b: (0, h))],
    )(
        joint,
        grad_mixture,
        cosine,
        sine,
        column,
        segments.reshape(blocks, 1, BLOCK),
    )


def result_kernel(where_ref, in_ref, got_ref, vec_ref, out_ref):
    width = in_ref.shape[1] // PIECES
    for r in range(PIECES):
        target = pl.ds(pl.multiple_of(where_ref[r] * width, width), width)
        at = slice(r * width, (r + 1) * width)
        total = got_ref[:, at].astype(F32) + in_ref[:, target].astype(F32) + vec_ref[4:5, at]
        out_ref[:, target] = total.astype(BF16)


def back_kernel(
    where_ref, in_ref, cot_ref, pad_ref, own_ref, below_ref, above_ref, out_ref, sum_ref
):
    x = in_ref[...].astype(F32)
    mean = jnp.mean(x, axis=1, keepdims=True)
    centred = x - mean
    inv = lax.rsqrt(jnp.mean(centred * centred, axis=1, keepdims=True) + EPS)
    features = x.shape[1]
    width = features // PIECES
    plain = jnp.zeros_like(mean)
    crossed = jnp.zeros_like(mean)
    for r in range(PIECES):
        target = pl.ds(pl.multiple_of(where_ref[r] * width, width), width)
        at = slice(r * width, (r + 1) * width)
        total = (
            own_ref[:, at].astype(F32)
            + below_ref[:, at].astype(F32)
            + above_ref[:, at].astype(F32)
        )
        sum_ref[:, at] = total
        plain += jnp.sum(total, axis=1, keepdims=True)
        normed = (in_ref[:, target].astype(F32) - mean) * inv
        crossed += jnp.sum(total * normed, axis=1, keepdims=True)
    plain = plain * (1.0 / features)
    crossed = crossed * (1.0 / features)
    marks = pad_ref[...].astype(F32)
    for r in range(PIECES):
        target = pl.ds(pl.multiple_of(where_ref[r] * width, width), width)
        at = slice(r * width, (r + 1) * width)
        normed = (in_ref[:, target].astype(F32) - mean) * inv
        seed = cot_ref[:, target].astype(F32) * marks
        out_ref[:, target] = (
            seed + inv * (sum_ref[:, at] - plain - normed * crossed)
        ).astype(BF16)


def finish(kernel, where, half, own_rows, got, tail, scratch=()):
    features = own_rows[0].shape[1]
    tile = got[0][1]
    row = (lambda at: at[PIECES]) if half is None else (lambda at: at[PIECES] * 2 + half)
    own = lambda w: pl.BlockSpec((tile, w), lambda i, at: (row(at), 0))
    here = lambda a: pl.BlockSpec(
        (tile, features), lambda i, at: (half if a.shape[0] > tile else 0, 0)
    )
    return call(
        kernel,
        shape(tile, features),
        20 * tile * features,
        12 * tile * features,
        grid_spec=pltpu.PrefetchScalarGridSpec(
            num_scalar_prefetch=1,
            grid=(1,),
            in_specs=[own(a.shape[1]) for a in own_rows]
            + [here(a) for a, _ in got]
            + [whole(*a.shape) for a in tail],
            out_specs=pl.BlockSpec((tile, features), lambda i, at: (0, 0)),
            scratch_shapes=[pltpu.VMEM((tile, features), F32)] * len(scratch),
        ),
    )(where, *own_rows, *(a for a, _ in got), *tail)


def swapped(a, bit):
    return lax.ppermute(a, "dp", [(i, i ^ bit) for i in range(PIECES)])


def crossed_over(from_x, from_y):
    core = lax.axis_index("dp") & 1
    pairs = [(i, i ^ (4 if i & 1 else 2)) for i in range(PIECES)]
    return lax.ppermute(jnp.where(core == 1, from_x, from_y), "dp", pairs)


def gather_pieces(items, after):
    gathered, arrived = {}, {}
    for name, own in items:
        if name in after:
            own, _ = lax.optimization_barrier((own, arrived[after[name]]))
        from_x = swapped(own, 2)
        from_y = swapped(own, 4)
        arrived[name] = (from_x, from_y)
        diagonal = crossed_over(from_x, from_y)
        near = (own, from_x, from_y, diagonal)
        far = [swapped(a, 1) for a in near]
        gathered[name] = [b for pair in zip(near, far) for b in pair]
    return gathered


def scattered_small(values):
    for bit in (4, 2, 1):
        values = values[:bit] + swapped(values[bit:], bit)
    return values[0]


def neighbours(t, spreading):
    n = lax.axis_size("mp")
    up = [(z, z + 1) for z in (range(t - 1, n - 1) if spreading else range(min(t, n - 1)))]
    return up, [(n - 1 - a, n - 1 - b) for a, b in up]


def summed_rows(part):
    n, me = lax.axis_size("mp"), lax.axis_index("mp")
    share = part.shape[0] // n
    tile = share // 2
    block = lambda j, half: lax.dynamic_slice_in_dim(
        part, jnp.clip(j, 0, n - 1) * share + half * tile, tile, 0
    )
    going = [(block(n - 1 + me, half), block(1 + me - n, half)) for half in (0, 1)]
    going = lax.optimization_barrier(going)
    got = [None, None]
    for t in range(1, n):
        up, down = neighbours(t, False)
        for half in (0, 1):
            if t > 1:
                pair = block(n - t + me, half), block(t + me - n, half)
                going[half] = lax.optimization_barrier(
                    tuple(mine + theirs for mine, theirs in zip(pair, got[half]))
                )
            got[half] = (
                lax.ppermute(going[half][0], "mp", up), lax.ppermute(going[half][1], "mp", down)
            )
    return got


def spread_rows(parts, room, late=None):
    n, me = lax.axis_size("mp"), lax.axis_index("mp")
    tile = parts[0].shape[0]
    rights, lefts = [parts], [parts]
    for t in range(1, n):
        up, down = neighbours(t, True)
        right, left = [], []
        if t == n - 1 and late is not None:
            rights[-1], lefts[-1], late = lax.optimization_barrier((rights[-1], lefts[-1], late))
        for i in range(len(parts)):
            right.append(lax.ppermute(rights[-1][i], "mp", up))
            left.append(lax.ppermute(lefts[-1][i], "mp", down))
        rights.append(right)
        lefts.append(left)
    for t in range(n):
        for i in range(len(parts)):
            rows = parts[i] if t == 0 else lefts[t][i] + rights[n - t][i]
            at = (lax.rem(me + t, n) * len(parts) + i) * tile
            room = lax.dynamic_update_slice_in_dim(room, rows, at, 0)
    return room, late


def summed_over_mp(values):
    n = lax.axis_size("mp")
    if n & (n - 1):
        return lax.psum(values, "mp")
    bit = 1
    while bit < n:
        pairs = [(z, z ^ bit) for z in range(n)]
        values = values + lax.ppermute(values, "mp", pairs)
        bit *= 2
    return values


def step(
    inputs,
    segments,
    padding,
    first_gain,
    first_shift,
    second_gain,
    second_shift,
    joint_weight,
    joint_bias,
    dense_weight,
    dense_bias,
    expand_weight,
    expand_bias,
    reduce_weight,
    reduce_bias,
    cotangent,
):
    total, features = inputs.shape
    n_dp = lax.axis_size("dp")
    dp_at, mp_at = lax.axis_index("dp"), lax.axis_index("mp")
    order = jnp.arange(PIECES, dtype=jnp.int32)
    small = (
        joint_bias, expand_bias, first_gain, first_shift, second_gain, second_shift,
        dense_bias, reduce_bias,
    )
    longest = max(a.shape[0] for a in small)
    line = lax.broadcasted_iota(jnp.int32, (len(small), longest), 0)
    packed = jnp.zeros((len(small), longest), BF16)
    for i, a in enumerate(small):
        packed = jnp.where(line == i, jnp.pad(a, (0, longest - a.shape[0]))[None], packed)
    if n_dp == PIECES:
        order = dp_at ^ order
        packed = packed[None]
        packed = jnp.concatenate([packed, swapped(packed, 1)], axis=0)
        packed = jnp.concatenate([packed] + [swapped(packed, bit) for bit in (2, 4, 6)], axis=0)
        blocks = gather_pieces(
            (
                ("D", dense_weight),
                ("E", expand_weight),
                ("J", joint_weight),
                ("R", reduce_weight),
            ),
            {"R": "J"},
        )
        dense, joint_w, wide, reduce = (blocks[k] for k in "DJER")
        padding, segments, packed = lax.optimization_barrier((padding, segments, packed))
        by_device = jnp.take(packed, order, axis=0)
    else:
        packed = by_device = lax.all_gather(packed, "dp")
        rows = lambda a: jnp.split(lax.all_gather(a, "dp", axis=0, tiled=True), PIECES, 0)
        columns = lambda a: jnp.split(lax.all_gather(a, "dp", axis=1, tiled=True), PIECES, 1)
        dense, joint_w = columns(dense_weight), rows(joint_weight)
        wide, reduce = rows(expand_weight), columns(reduce_weight)
    where = jnp.concatenate([order, mp_at[None].astype(jnp.int32)])
    taken = lambda a, i: a[:, i, : small[i].shape[0]].reshape(1, -1).astype(F32)
    bias_j, bias_e = taken(by_device, 0), taken(by_device, 1)
    vectors = jnp.concatenate(
        [taken(packed, i) for i in range(2, 6)]
        + [taken(packed, 6) + taken(packed, 7), jnp.zeros((3, features), F32)]
    )

    marks = padding[:, None]
    hidden_one, hidden_two, normed, seed, bias_back = rows_pass(
        where, inputs, cotangent, marks, vectors
    )
    cosine, sine = rotary_tables(segments)
    column = segments.reshape(total, 1)
    cosine, sine, column, hidden_two = lax.optimization_barrier(
        (cosine, sine, column, hidden_two)
    )

    grad_mixture = mixture_back(seed, dense)
    joint = project(hidden_one, joint_w, bias_j)
    mixture, joint_low, joint_bias_back = attend(joint, grad_mixture, cosine, sine, column, segments)
    activated, slope = expand(hidden_two, wide, bias_e)
    branch = branch_of(mixture, activated, dense, reduce)
    before_low, expand_bias_back = before_back(seed, reduce, slope)
    gx, gains = gx_of(joint_low, before_low, normed, vectors, joint_w, wide)

    tile = total // lax.axis_size("mp") // 2
    branches = lax.psum_scatter(branch, "mp", scatter_dimension=0, tiled=True)
    result = finish(
        result_kernel, where, None, (inputs,), ((branches, 2 * tile),),
        (vectors,),
    )
    result, _ = spread_rows([result], branch)
    grads = gradient(
        where, (hidden_one, seed, hidden_two, seed),
        (joint_low, mixture, before_low, activated),
    )
    grads, _ = lax.optimization_barrier((grads, branches))
    grads = lax.psum_scatter(grads, "dp", scatter_dimension=0, tiled=True)
    cuts = [0]
    for a in (joint_low, mixture, before_low, activated):
        cuts.append(cuts[-1] + a.shape[1])
    piece = lambda i: grads[:, cuts[i] : cuts[i + 1]].astype(F32)
    weights = (piece(0), piece(1).T, piece(2), piece(3).T)

    back = [
        finish(back_kernel, where, half, (inputs, cotangent, marks, gx),
              tuple((a, tile) for a in got), (), (0,))
        for half, got in enumerate(summed_rows(gx))
    ]
    back, weights = spread_rows(back, gx, weights)

    gains = jnp.sum(gains.reshape(4, 8, features), axis=1)
    gains = summed_over_mp(gains)
    straight = jnp.concatenate([gains, jnp.sum(bias_back, axis=0)[None]])
    by_row = [
        jnp.sum(joint_bias_back, axis=0).reshape(n_dp, -1),
        jnp.sum(expand_bias_back, axis=0).reshape(n_dp, -1),
    ]
    if n_dp == PIECES:
        by_row = [jnp.take(a, order, axis=0) for a in by_row]
    sums = jnp.concatenate(
        by_row + [straight[i].reshape(n_dp, -1) for i in range(5)], axis=1
    )
    if n_dp == PIECES:
        sums = scattered_small(sums)
    else:
        sums = lax.psum_scatter(sums, "dp", scatter_dimension=0, tiled=True).reshape(-1)
    widths = [joint_bias.shape[0], expand_bias.shape[0]] + [features // n_dp] * 5
    cuts = [sum(widths[:i]) for i in range(len(widths) + 1)]
    parts = [sums[a:b] for a, b in zip(cuts, cuts[1:])]
    return (
        result, back, parts[2], parts[3], parts[4], parts[5],
        weights[0], parts[0], weights[1], parts[6],
        weights[2], parts[1], weights[3], parts[6],
    )


def solution(mesh):
    placed = (
        P("dp", None), P("dp"), P("dp"), P("dp"), P("dp"), P("dp"), P("dp"),
        P("dp", "mp"), P(("mp", "dp")), P("mp", "dp"), P("dp"),
        P("dp", "mp"), P(("mp", "dp")), P("mp", "dp"), P("dp"), P("dp", None),
    )
    return jax.shard_map(
        step,
        mesh=mesh,
        in_specs=placed,
        out_specs=(
            P("dp", None), P("dp", None), P("dp"), P("dp"), P("dp"), P("dp"),
            P("dp", "mp"), P(("mp", "dp")), P("mp", "dp"), P("dp"),
            P("dp", "mp"), P(("mp", "dp")), P("mp", "dp"), P("dp"),
        ),
        check_vma=False,
    )
```

time: 908 us -> 574 us (0.63)
  waiting for transfers between devices: 487 us -> 210 us
  matrix products: 184 us -> 0 us
  Pallas kernels: 0 us -> 164 us
  starting transfers between devices: 0.36 us -> 109 us
  blocking collectives: 100 us -> 0 us
  other arithmetic: 66.2 us -> 46.9 us
  local copies, waits for them, and re-layouts: 44.1 us -> 26.5 us
    psum x1 -> x0, waiting for transfers between devices: 396 us -> none  [shards(): lax.psum(branch_part.astype(jnp.bfloat16), 'mp').astype(jnp.float32)]
    dot_general x36 -> x0, matrix products: 184 us -> none  [the longest x2 24.8 us: shards(): jnp.dot(activated.T, seed_low, preferred_element_type=jnp.float32)]
    ppermute x0 -> x67, waiting for transfers between devices: none -> 183 us  [the longest x9 62.9 us: spread_rows(): left.append(lax.ppermute(lefts[-1][i], 'mp', down))]
    pallas_call x0 -> x12, Pallas kernels: none -> 164 us  [the longest x1 35.8 us: gradient(): call(gradient_kernel, shape(features, width), 2 * total * features * widt...]
    ppermute x0 -> x67, starting transfers between devices: none -> 109 us  [the longest x6 28.2 us: summed_rows(): lax.ppermute(going[half][0], 'mp', up)]
    reduce_scatter x4 -> x2, waiting for transfers between devices: 88.9 us -> 27 us  [the longest x1 27 us: step(): branches = lax.psum_scatter(branch, 'mp', scatter_dimension=0, tiled=True)]
    all_gather x7 -> x0, blocking collectives: 59.3 us -> none  [the longest x1 8.89 us: shards(): lax.all_gather(first_shift, 'dp', axis=0, tiled=True)]
    unnamed x2 -> x0, blocking collectives: 40.9 us -> none
  transfers between devices with their start and end apart: 9 -> 69, of which waited for: 3 -> 20; matrix products, arithmetic and copies ran while one was open for 31% -> 12% of each run, Pallas kernels for 0% -> 26%
where the time goes in v1:
time: 574 us; the launch traced here: 572 us
  waiting for transfers between devices  210 us (37%)
  Pallas kernels  164 us (29%)
  starting transfers between devices  109 us (19%)
  other arithmetic  46.9 us (8%)
  local copies, waits for them, and re-layouts  26.5 us (5%)
  between operations  15.1 us (3%)
    ppermute x9, waiting for transfers between devices, spread_rows(): left.append(lax.ppermute(lefts[-1][i], 'mp', down))  62.9 us
    ppermute x4, waiting for transfers between devices, crossed_over(): return lax.ppermute(jnp.where(core == 1, from_x, from_y), 'dp', pairs)  47.9 us
    pallas_call x1, Pallas kernels, gradient(): call(gradient_kernel, shape(features, width), 2 * total * features * widt...  35.8 us
    ppermute x6, waiting for transfers between devices, summed_rows(): lax.ppermute(going[half][0], 'mp', up)  30.5 us
    ppermute x31, waiting for transfers between devices, swapped(): return lax.ppermute(a, 'dp', [(i, i ^ bit) for i in range(PIECES)])  29.3 us
    ppermute x6, starting transfers between devices, summed_rows(): lax.ppermute(going[half][0], 'mp', up)  28.2 us
    ppermute x9, starting transfers between devices, spread_rows(): right.append(lax.ppermute(rights[-1][i], 'mp', up))  27.8 us
    reduce_scatter x1, waiting for transfers between devices, step(): branches = lax.psum_scatter(branch, 'mp', scatter_dimension=0, tiled=True)  27 us
  transfers between devices with their start and end apart: 69, of which 20 were waited for; matrix products, arithmetic and copies ran while one was open for 12% of the time, Pallas kernels for 26%

profile of v1, /device:TPU:0, one launch (start us, length us, event | category | flops | bytes accessed | tf_op | source)
XLA Modules:
  0.0 571.6 jit_solution(6556271009285423918)
XLA Ops:
  20.5 13.4 %collective-permute-done.2 = bf16[2,8,256]{2,1,0:T(8,128)(2,1)S(1)} collective-permute-done((bf16[2,8,256]{2,1,0:T(8,128)(2,1)S(1)}, bf16[2,8,256]{2,1,0:T(8,128)(2,1)S(1)}, u32[]{:S(2)}, u32[]{:S(2)}) %collective-permute-start.2) | collective-permute-done | bytes 8224 | tf_op jit(solution)/shard_map/ppermute | solution.py:519
  48.8 10.4 %collective-permute-done.5.refs_3_.refs_6_ = bf16[256,1536]{1,0:T(8,128)(2,1)} collective-permute-done((bf16[256,1536]{1,0:T(8,128)(2,1)}, bf16[256,1536]{1,0:T(8,128)(2,1)}, u32[]{:S(2)}, u32[]{:S(2)}) %collective-permute-start.5) | collective-permute-done | bytes 786464 | tf_op jit(solution)/shard_map/ppermute | solution.py:519
  63.7 23.4 %collective-permute-done.16.refs_7_.refs_8_ = bf16[512,256]{1,0:T(8,128)(2,1)S(1)} collective-permute-done((bf16[512,256]{1,0:T(8,128)(2,1)S(1)}, bf16[512,256]{1,0:T(8,128)(2,1)S(1)}, u32[]{:S(2)}, u32[]{:S(2)}) %collective-permute-start.16) | collective-permute-done | bytes 262176 | tf_op jit(solution)/shard_map/ppermute | solution.py:525
  92.2 20.3 %collective-permute-done.9.refs_7_.refs_10_ = bf16[256,1536]{1,0:T(8,128)(2,1)} collective-permute-done((bf16[256,1536]{1,0:T(8,128)(2,1)S(1)}, bf16[256,1536]{1,0:T(8,128)(2,1)}, u32[]{:S(2)}, u32[]{:S(2)}) %collective-permute-start.9) | collective-permute-done | bytes 786464 | tf_op jit(solution)/shard_map/ppermute | solution.py:525
  125.2 14.3 %shard_map.263 = (bf16[1024,2048]{1,0:T(8,128)(2,1)}, bf16[1024,2048]{1,0:T(8,128)(2,1)}, bf16[1024,2048]{1,0:T(8,128)(2,1)}, bf16[1024,2048]{1,0:T(8,128)(2,1)}, f32[8,2048]{1,0:T(8,128)}) custom-call(s32[9]{0:T(128)} %pad_add_fusion.where_ref, bf16[1024,2048]{1,0:T(8,128)(2,1)} %in_ref.7, bf16[1024,2048]{1,0:T(8,128)(2,1)} %cot_ref.5, ...), custom_call_target="tpu_custom_call" | custom-call | flops 83886080 | bytes 25165824 | tf_op jit(solution)/shard_map/pallas_call | solution.py:96
  141.6 6.2 %shard_map.265.grad_ref = bf16[1024,512]{1,0:T(8,128)(2,1)} custom-call(bf16[1024,2048]{1,0:T(8,128)(2,1)} %get-tuple-element.60.refs_0_.refs_1_.refs_3_, bf16[512,256]{1,0:T(8,128)(2,1)} %refs_2_.1, bf16[512,256]{1,0:T(8,128)(2,1)} %collective-permute-done.11.refs_2_.refs_3_, bf16[512,256]{1,0:T(8,128)(2,1)} %collective-permute-done.12.refs_3_.refs_4_, ...), custom_call_target="tpu_custom_call" | custom-call | flops 2147483648 | bytes 7340032 | tf_op jit(solution)/shard_map/pallas_call | solution.py:175
  147.8 11.8 %shard_map.264.joint_ref = f32[1024,1536]{1,0:T(8,128)} custom-call(bf16[1024,2048]{1,0:T(8,128)(2,1)} %get-tuple-element.59.refs_0_, bf16[256,1536]{1,0:T(8,128)(2,1)} %refs_4_.1, bf16[256,1536]{1,0:T(8,128)(2,1)} %collective-permute-done.4.refs_2_.refs_5_, bf16[256,1536]{1,0:T(8,128)(2,1)} %collective-permute-done.5.refs_3_.refs_6_, ...), custom_call_target="tpu_custom_call" | custom-call | flops 6442450944 | bytes 16777216 | tf_op jit(solution)/shard_map/pallas_call | solution.py:125
  160.8 11.7 %shard_map.266 = (bf16[1024,512]{1,0:T(8,128)(2,1)}, bf16[1024,1536]{1,0:T(8,128)(2,1)}, f32[8,1536]{1,0:T(8,128)}) custom-call(f32[1024,1536]{1,0:T(8,128)} %shard_map.264.joint_ref, bf16[1024,512]{1,0:T(8,128)(2,1)} %shard_map.265.grad_ref, f32[1024,128]{1,0:T(8,128)} %maximum_maximum_fusion.cos_ref, f32[1024,128]{1,0:T(8,128)} %maximum_maximum_fusion.1.sin_ref, ...), custom_call_target="tpu_custom_call" | custom-call | flops 3758096384 | bytes 12582912 | tf_op jit(solution)/shard_map/pallas_call | solution.py:422
  173.5 16.6 %shard_map.267 = (bf16[1024,2048]{1,0:T(8,128)(2,1)}, bf16[1024,2048]{1,0:T(8,128)(2,1)}) custom-call(bf16[1024,2048]{1,0:T(8,128)(2,1)} %get-tuple-element.67.refs_0_.refs_2_, bf16[256,2048]{1,0:T(8,128)(2,1)} %refs_12_.1, bf16[256,2048]{1,0:T(8,128)(2,1)} %collective-permute-done.18.refs_2_.refs_13_, bf16[256,2048]{1,0:T(8,128)(2,1)} %copy-done.6, ...), custom_call_target="tpu_custom_call" | custom-call | flops 8589934592 | bytes 20971520 | tf_op jit(solution)/shard_map/pallas_call | solution.py:151
  192.1 16.8 %shard_map.268 = bf16[1024,2048]{1,0:T(8,128)(2,1)} custom-call(bf16[1024,512]{1,0:T(8,128)(2,1)} %get-tuple-element.66.refs_0_.refs_5_, bf16[1024,2048]{1,0:T(8,128)(2,1)} %get-tuple-element.68.refs_1_.refs_7_, bf16[512,256]{1,0:T(8,128)(2,1)} %refs_2_.1, bf16[512,256]{1,0:T(8,128)(2,1)} %collective-permute-done.11.refs_2_.refs_3_, ...), custom_call_target="tpu_custom_call" | custom-call | flops 10737418240 | bytes 19922944 | tf_op jit(solution)/shard_map/pallas_call | solution.py:259
  209.0 14.5 %shard_map.270 = (bf16[1024,2048]{1,0:T(8,128)(2,1)}, f32[8,2048]{1,0:T(8,128)}) custom-call(bf16[1024,2048]{1,0:T(8,128)(2,1)} %get-tuple-element.60.refs_0_.refs_1_.refs_3_, bf16[2048,256]{1,0:T(8,128)(2,1)} %refs_1_.6, bf16[2048,256]{1,0:T(8,128)(2,1)} %copy-done.19, bf16[2048,256]{1,0:T(8,128)(2,1)} %collective-permute-done.26.refs_12_.refs_3_, ...), custom_call_target="tpu_custom_call" | custom-call | flops 8589934592 | bytes 20971520 | tf_op jit(solution)/shard_map/pallas_call | solution.py:199
  223.5 35.8 %shard_map.274 = bf16[2048,6144]{1,0:T(8,128)(2,1)} custom-call(s32[9]{0:T(128)} %pad_add_fusion.where_ref, bf16[1024,2048]{1,0:T(8,128)(2,1)} %get-tuple-element.59.refs_0_, bf16[1024,2048]{1,0:T(8,128)(2,1)} %get-tuple-element.60.refs_0_.refs_1_.refs_3_, bf16[1024,2048]{1,0:T(8,128)(2,1)} %get-tuple-element.67.refs_0_.refs_2_, ...), custom_call_target="tpu_custom_call" | custom-call | flops 25769803776 | bytes 54525952 | tf_op jit(solution)/shard_map/pallas_call | solution.py:327
  259.3 27.0 %reduce-scatter.3.cloned.1.call-done.got_ref = bf16[256,2048]{1,0:T(8,128)(2,1)} async-done(((bf16[1024,2048]{1,0:T(8,128)(2,1)}), bf16[256,2048]{1,0:T(8,128)(2,1)}) %reduce-scatter.3.cloned.1.call-update) | async-done | bytes 1048592 | tf_op jit(solution)/shard_map/reduce_scatter | solution.py:694
  286.4 24.2 %shard_map.271 = (bf16[1024,2048]{1,0:T(8,128)(2,1)}, f32[32,2048]{1,0:T(8,128)}) custom-call(bf16[1024,1536]{1,0:T(8,128)(2,1)} %get-tuple-element.70.refs_0_.refs_4_, bf16[1024,2048]{1,0:T(8,128)(2,1)} %get-tuple-element.72.refs_1_.refs_6_, bf16[1024,2048]{1,0:T(8,128)(2,1)} %get-tuple-element.73.refs_2_, f32[8,2048]{1,0:T(8,128)} %concatenate.25.vec_ref.refs_3_, ...), custom_call_target="tpu_custom_call" | custom-call | flops 15032385536 | bytes 30408704 | tf_op jit(solution)/shard_map/pallas_call | solution.py:292
  323.6 6.3 %collective-permute-done.38 = bf16[128,2048]{1,0:T(8,128)(2,1)S(1)} collective-permute-done((bf16[128,2048]{1,0:T(8,128)(2,1)}, bf16[128,2048]{1,0:T(8,128)(2,1)S(1)}, u32[]{:S(2)}, u32[]{:S(2)}) %collective-permute-start.38) | collective-permute-done | bytes 524320 | tf_op jit(solution)/shard_map/ppermute | solution.py:574
  332.5 5.1 collective-permute-start.40
  339.8 4.3 collective-permute-start.63
  344.1 8.7 %collective-permute-done.63 = f32[4,2048]{1,0:T(4,128)S(1)} collective-permute-done((f32[4,2048]{1,0:T(4,128)S(1)}, f32[4,2048]{1,0:T(4,128)S(1)}, u32[]{:S(2)}, u32[]{:S(2)}) %collective-permute-start.63) | collective-permute-done | bytes 32800 | tf_op jit(solution)/shard_map/ppermute | solution.py:608
  358.2 6.4 %collective-permute-start.33 = (bf16[256,2048]{1,0:T(8,128)(2,1)}, bf16[256,2048]{1,0:T(8,128)(2,1)S(1)}, u32[]{:S(2)}, u32[]{:S(2)}) collective-permute-start(bf16[256,2048]{1,0:T(8,128)(2,1)} %shard_map.269), channel_id=1, source_target_pairs={{0,1},{1,2},{2,3},{4,5},{5,6},{6,7},{8,9},{9,10},{10,11},{12,13},{... | collective-permute-start | bytes 3145736 | tf_op jit(solution)/shard_map/ppermute | solution.py:589
  372.2 4.6 collective-permute-start.46
  378.4 21.1 %collective-permute-done.42.below_ref = bf16[128,2048]{1,0:T(8,128)(2,1)S(1)} collective-permute-done((bf16[128,2048]{1,0:T(8,128)(2,1)S(1)}, bf16[128,2048]{1,0:T(8,128)(2,1)S(1)}, u32[]{:S(2)}, u32[]{:S(2)}) %collective-permute-start.42) | collective-permute-done | bytes 524320 | tf_op jit(solution)/shard_map/ppermute | solution.py:574
  402.4 4.8 copy.60
  407.4 4.4 shard_map.272
  415.6 9.4 %collective-permute-start.48 = (bf16[128,2048]{1,0:T(8,128)(2,1)}, bf16[128,2048]{1,0:T(8,128)(2,1)}, u32[]{:S(2)}, u32[]{:S(2)}) collective-permute-start(bf16[128,2048]{1,0:T(8,128)(2,1)} %get-tuple-element.85), channel_id=1, source_target_pairs={{0,1},{1,2},{2,3},{4,5},{5,6},{6,7},{8,9},{9,10},{10,11},{12,13},{... | collective-permute-start | bytes 1572872 | tf_op jit(solution)/shard_map/ppermute | solution.py:574
  426.2 5.3 collective-permute-start.51
  441.7 4.5 shard_map.273
  447.5 7.9 %collective-permute-start.53 = (bf16[128,2048]{1,0:T(8,128)(2,1)}, bf16[128,2048]{1,0:T(8,128)(2,1)S(1)}, u32[]{:S(2)}, u32[]{:S(2)}) collective-permute-start(bf16[128,2048]{1,0:T(8,128)(2,1)} %shard_map.273), channel_id=1, source_target_pairs={{0,1},{1,2},{2,3},{4,5},{5,6},{6,7},{8,9},{9,10},{10,11},{12,13},{... | collective-permute-start | bytes 1572872 | tf_op jit(solution)/shard_map/ppermute | solution.py:589
  459.6 15.9 %collective-permute-done.50 = bf16[128,2048]{1,0:T(8,128)(2,1)} collective-permute-done((bf16[128,2048]{1,0:T(8,128)(2,1)S(1)}, bf16[128,2048]{1,0:T(8,128)(2,1)}, u32[]{:S(2)}, u32[]{:S(2)}) %collective-permute-start.50) | collective-permute-done | bytes 524320 | tf_op jit(solution)/shard_map/ppermute | solution.py:590
  476.9 8.7 %collective-permute-done.56 = bf16[128,2048]{1,0:T(8,128)(2,1)} collective-permute-done((bf16[128,2048]{1,0:T(8,128)(2,1)}, bf16[128,2048]{1,0:T(8,128)(2,1)}, u32[]{:S(2)}, u32[]{:S(2)}) %collective-permute-start.56) | collective-permute-done | bytes 524320 | tf_op jit(solution)/shard_map/ppermute | solution.py:590
  503.4 10.4 %collective-permute-done.57 = bf16[128,2048]{1,0:T(8,128)(2,1)} collective-permute-done((bf16[128,2048]{1,0:T(8,128)(2,1)}, bf16[128,2048]{1,0:T(8,128)(2,1)}, u32[]{:S(2)}, u32[]{:S(2)}) %collective-permute-start.57) | collective-permute-done | bytes 524320 | tf_op jit(solution)/shard_map/ppermute | solution.py:590
  516.7 17.6 %collective-permute-done.37 = bf16[256,2048]{1,0:T(8,128)(2,1)} collective-permute-done((bf16[256,2048]{1,0:T(8,128)(2,1)}, bf16[256,2048]{1,0:T(8,128)(2,1)}, u32[]{:S(2)}, u32[]{:S(2)}) %collective-permute-start.37) | collective-permute-done | bytes 1048608 | tf_op jit(solution)/shard_map/ppermute | solution.py:590
  557.0 6.2 %collective-permute-done.61 = bf16[128,2048]{1,0:T(8,128)(2,1)S(1)} collective-permute-done((bf16[128,2048]{1,0:T(8,128)(2,1)}, bf16[128,2048]{1,0:T(8,128)(2,1)S(1)}, u32[]{:S(2)}, u32[]{:S(2)}) %collective-permute-start.61) | collective-permute-done | bytes 524320 | tf_op jit(solution)/shard_map/ppermute | solution.py:590
  (268 shorter events, 158.6 us)
Async XLA Ops:
  7.2 279.1 %reduce-scatter.3.cloned.1.call-start = ((), (), s32[]{:S(2)}) async-start(), calls=%async_computation.2 | async-start | bytes 5242880 | tf_op jit(solution)/shard_map/reduce_scatter | solution.py:694
  7.2 36.2 %collective-permute-start.14 = (bf16[512,256]{1,0:T(8,128)(2,1)}, bf16[512,256]{1,0:T(8,128)(2,1)S(1)}, u32[]{:S(2)}, u32[]{:S(2)}) collective-permute-start(bf16[512,256]{1,0:T(8,128)(2,1)} %refs_2_.1), channel_id=1, source_target_pairs={{0,16},{4,20},{8,24},{12,28},{16,0},{20,4},{24,8},{28,12},{1,17},{... | collective-permute-start | bytes 786440 | tf_op jit(solution)/shard_map/ppermute | solution.py:519
  10.3 34.8 %collective-permute-start.12 = (bf16[512,256]{1,0:T(8,128)(2,1)}, bf16[512,256]{1,0:T(8,128)(2,1)}, u32[]{:S(2)}, u32[]{:S(2)}) collective-permute-start(bf16[512,256]{1,0:T(8,128)(2,1)} %refs_2_.1), channel_id=1, source_target_pairs={{0,8},{4,12},{8,0},{12,4},{16,24},{20,28},{24,16},{28,20},{1,9},{5... | collective-permute-start | bytes 786440 | tf_op jit(solution)/shard_map/ppermute | solution.py:519
  11.8 47.4 %collective-permute-start.11 = (bf16[512,256]{1,0:T(8,128)(2,1)}, bf16[512,256]{1,0:T(8,128)(2,1)}, u32[]{:S(2)}, u32[]{:S(2)}) collective-permute-start(bf16[512,256]{1,0:T(8,128)(2,1)} %refs_2_.1), channel_id=1, source_target_pairs={{0,4},{4,0},{8,12},{12,8},{16,20},{20,16},{24,28},{28,24},{1,5},{5... | collective-permute-start | bytes 786440 | tf_op jit(solution)/shard_map/ppermute | solution.py:519
  13.9 33.3 %collective-permute-start.7 = (bf16[256,1536]{1,0:T(8,128)(2,1)}, bf16[256,1536]{1,0:T(8,128)(2,1)}, u32[]{:S(2)}, u32[]{:S(2)}) collective-permute-start(bf16[256,1536]{1,0:T(8,128)(2,1)} %refs_4_.1), channel_id=1, source_target_pairs={{0,16},{4,20},{8,24},{12,28},{16,0},{20,4},{24,8},{28,12},{1,17},{... | collective-permute-start | bytes 2359304 | tf_op jit(solution)/shard_map/ppermute | solution.py:519
  43.5 45.4 %collective-permute-start.21 = (bf16[256,2048]{1,0:T(8,128)(2,1)}, bf16[256,2048]{1,0:T(8,128)(2,1)S(1)}, u32[]{:S(2)}, u32[]{:S(2)}) collective-permute-start(bf16[256,2048]{1,0:T(8,128)(2,1)} %refs_12_.1), channel_id=1, source_target_pairs={{0,16},{4,20},{8,24},{12,28},{16,0},{20,4},{24,8},{28,12},{1,17},{... | collective-permute-start | bytes 3145736 | tf_op jit(solution)/shard_map/ppermute | solution.py:519
  45.1 43.9 %collective-permute-start.19 = (bf16[256,2048]{1,0:T(8,128)(2,1)}, bf16[256,2048]{1,0:T(8,128)(2,1)S(1)}, u32[]{:S(2)}, u32[]{:S(2)}) collective-permute-start(bf16[256,2048]{1,0:T(8,128)(2,1)} %refs_12_.1), channel_id=1, source_target_pairs={{0,8},{4,12},{8,0},{12,4},{16,24},{20,28},{24,16},{28,20},{1,9},{5... | collective-permute-start | bytes 3145736 | tf_op jit(solution)/shard_map/ppermute | solution.py:519
  47.2 39.9 %collective-permute-start.16 = (bf16[512,256]{1,0:T(8,128)(2,1)S(1)}, bf16[512,256]{1,0:T(8,128)(2,1)S(1)}, u32[]{:S(2)}, u32[]{:S(2)}) collective-permute-start(bf16[512,256]{1,0:T(8,128)(2,1)S(1)} %broadcast_select_fusion.3), channel_id=1, source_target_pairs={{0,8},{4,20},{8,0},{12,28},{16,24},{20,4},{24,16},{28,12},{1,9},{5... | collective-permute-start | bytes 786440 | tf_op jit(solution)/shard_map/ppermute | solution.py:525
  59.1 53.4 %collective-permute-start.28 = (bf16[2048,256]{1,0:T(8,128)(2,1)}, bf16[2048,256]{1,0:T(8,128)(2,1)}, u32[]{:S(2)}, u32[]{:S(2)}) collective-permute-start(bf16[2048,256]{1,0:T(8,128)(2,1)} %refs_1_.6), channel_id=1, source_target_pairs={{0,16},{4,20},{8,24},{12,28},{16,0},{20,4},{24,8},{28,12},{1,17},{... | collective-permute-start | bytes 3145736 | tf_op jit(solution)/shard_map/ppermute | solution.py:519
  62.1 50.9 %collective-permute-start.26 = (bf16[2048,256]{1,0:T(8,128)(2,1)}, bf16[2048,256]{1,0:T(8,128)(2,1)}, u32[]{:S(2)}, u32[]{:S(2)}) collective-permute-start(bf16[2048,256]{1,0:T(8,128)(2,1)} %refs_1_.6), channel_id=1, source_target_pairs={{0,8},{4,12},{8,0},{12,4},{16,24},{20,28},{24,16},{28,20},{1,9},{5... | collective-permute-start | bytes 3145736 | tf_op jit(solution)/shard_map/ppermute | solution.py:519
  90.7 33.0 %collective-permute-start.23 = (bf16[256,2048]{1,0:T(8,128)(2,1)}, bf16[256,2048]{1,0:T(8,128)(2,1)}, u32[]{:S(2)}, u32[]{:S(2)}) collective-permute-start(bf16[256,2048]{1,0:T(8,128)(2,1)} %broadcast_select_fusion.1), channel_id=1, source_target_pairs={{0,8},{4,20},{8,0},{12,28},{16,24},{20,4},{24,16},{28,12},{1,9},{5... | collective-permute-start | bytes 3145736 | tf_op jit(solution)/shard_map/ppermute | solution.py:525
  118.5 41.1 %collective-permute-start.18 = (bf16[256,2048]{1,0:T(8,128)(2,1)}, bf16[256,2048]{1,0:T(8,128)(2,1)}, u32[]{:S(2)}, u32[]{:S(2)}) collective-permute-start(bf16[256,2048]{1,0:T(8,128)(2,1)} %refs_12_.1), channel_id=1, source_target_pairs={{0,4},{4,0},{8,12},{12,8},{16,20},{20,16},{24,28},{28,24},{1,5},{5... | collective-permute-start | bytes 3145736 | tf_op jit(solution)/shard_map/ppermute | solution.py:519
  119.1 41.1 %collective-permute-start.22 = (bf16[256,2048]{1,0:T(8,128)(2,1)S(1)}, bf16[256,2048]{1,0:T(8,128)(2,1)}, u32[]{:S(2)}, u32[]{:S(2)}) collective-permute-start(bf16[256,2048]{1,0:T(8,128)(2,1)S(1)} %collective-permute-done.21.refs_5_.refs_16_), channel_id=1, source_target_pairs={{0,4},{4,0},{8,12},{12,8},{16,20},{20,16},{24,28},{28,24},{1,5},{5... | collective-permute-start | bytes 3145736 | tf_op jit(solution)/shard_map/ppermute | solution.py:519
  119.2 41.1 %collective-permute-start.20 = (bf16[256,2048]{1,0:T(8,128)(2,1)S(1)}, bf16[256,2048]{1,0:T(8,128)(2,1)}, u32[]{:S(2)}, u32[]{:S(2)}) collective-permute-start(bf16[256,2048]{1,0:T(8,128)(2,1)S(1)} %collective-permute-done.19.refs_3_.refs_14_), channel_id=1, source_target_pairs={{0,4},{4,0},{8,12},{12,8},{16,20},{20,16},{24,28},{28,24},{1,5},{5... | collective-permute-start | bytes 3145736 | tf_op jit(solution)/shard_map/ppermute | solution.py:519
  123.7 37.0 %collective-permute-start.30 = (bf16[2048,256]{1,0:T(8,128)(2,1)}, bf16[2048,256]{1,0:T(8,128)(2,1)}, u32[]{:S(2)}, u32[]{:S(2)}) collective-permute-start(bf16[2048,256]{1,0:T(8,128)(2,1)} %broadcast_select_fusion), channel_id=1, source_target_pairs={{0,8},{4,20},{8,0},{12,28},{16,24},{20,4},{24,16},{28,12},{1,9},{5... | collective-permute-start | bytes 3145736 | tf_op jit(solution)/shard_map/ppermute | solution.py:525
  209.0 287.5 %reduce-scatter.5.cloned.1.call-start = ((), (), s32[]{:S(2)}) async-start(), calls=%async_computation.3 | async-start | bytes 28311552 | tf_op jit(solution)/shard_map/reduce_scatter | solution.py:705
  318.9 39.2 %collective-permute-start.44 = (bf16[128,2048]{1,0:T(8,128)(2,1)S(1)}, bf16[128,2048]{1,0:T(8,128)(2,1)S(1)}, u32[]{:S(2)}, u32[]{:S(2)}) collective-permute-start(bf16[128,2048]{1,0:T(8,128)(2,1)S(1)} %get-tuple-element.81), channel_id=1, source_target_pairs={{0,1},{4,5},{8,9},{12,13},{16,17},{20,21},{24,25},{28,29}} | collective-permute-start | bytes 1572872 | tf_op jit(solution)/shard_map/ppermute | solution.py:574
  322.9 41.7 %collective-permute-start.45 = (bf16[128,2048]{1,0:T(8,128)(2,1)}, bf16[128,2048]{1,0:T(8,128)(2,1)S(1)}, u32[]{:S(2)}, u32[]{:S(2)}) collective-permute-start(bf16[128,2048]{1,0:T(8,128)(2,1)} %get-tuple-element.82), channel_id=1, source_target_pairs={{3,2},{7,6},{11,10},{15,14},{19,18},{23,22},{27,26},{31,30}} | collective-permute-start | bytes 1572872 | tf_op jit(solution)/shard_map/ppermute | solution.py:574
  332.5 32.1 %collective-permute-start.40 = (bf16[128,2048]{1,0:T(8,128)(2,1)}, bf16[128,2048]{1,0:T(8,128)(2,1)}, u32[]{:S(2)}, u32[]{:S(2)}) collective-permute-start(bf16[128,2048]{1,0:T(8,128)(2,1)} %get-tuple-element.77), channel_id=1, source_target_pairs={{0,1},{1,2},{4,5},{5,6},{8,9},{9,10},{12,13},{13,14},{16,17},{17,1... | collective-permute-start | bytes 1572872 | tf_op jit(solution)/shard_map/ppermute | solution.py:574
  358.2 42.6 %collective-permute-start.33 = (bf16[256,2048]{1,0:T(8,128)(2,1)}, bf16[256,2048]{1,0:T(8,128)(2,1)S(1)}, u32[]{:S(2)}, u32[]{:S(2)}) collective-permute-start(bf16[256,2048]{1,0:T(8,128)(2,1)} %shard_map.269), channel_id=1, source_target_pairs={{0,1},{1,2},{2,3},{4,5},{5,6},{6,7},{8,9},{9,10},{10,11},{12,13},{... | collective-permute-start | bytes 3145736 | tf_op jit(solution)/shard_map/ppermute | solution.py:589
  367.5 31.9 %collective-permute-start.42 = (bf16[128,2048]{1,0:T(8,128)(2,1)S(1)}, bf16[128,2048]{1,0:T(8,128)(2,1)S(1)}, u32[]{:S(2)}, u32[]{:S(2)}) collective-permute-start(bf16[128,2048]{1,0:T(8,128)(2,1)S(1)} %get-tuple-element.79), channel_id=1, source_target_pairs={{0,1},{1,2},{2,3},{4,5},{5,6},{6,7},{8,9},{9,10},{10,11},{12,13},{... | collective-permute-start | bytes 1572872 | tf_op jit(solution)/shard_map/ppermute | solution.py:574
  371.0 36.3 %collective-permute-start.43 = (bf16[128,2048]{1,0:T(8,128)(2,1)}, bf16[128,2048]{1,0:T(8,128)(2,1)}, u32[]{:S(2)}, u32[]{:S(2)}) collective-permute-start(bf16[128,2048]{1,0:T(8,128)(2,1)} %get-tuple-element.80), channel_id=1, source_target_pairs={{3,2},{2,1},{1,0},{7,6},{6,5},{5,4},{11,10},{10,9},{9,8},{15,14},{... | collective-permute-start | bytes 1572872 | tf_op jit(solution)/shard_map/ppermute | solution.py:574
  372.2 39.6 %collective-permute-start.46 = (bf16[128,2048]{1,0:T(8,128)(2,1)}, bf16[128,2048]{1,0:T(8,128)(2,1)S(1)}, u32[]{:S(2)}, u32[]{:S(2)}) collective-permute-start(bf16[128,2048]{1,0:T(8,128)(2,1)} %get-tuple-element.83), channel_id=1, source_target_pairs={{0,1},{1,2},{4,5},{5,6},{8,9},{9,10},{12,13},{13,14},{16,17},{17,1... | collective-permute-start | bytes 1572872 | tf_op jit(solution)/shard_map/ppermute | solution.py:574
  376.8 35.8 %collective-permute-start.47 = (bf16[128,2048]{1,0:T(8,128)(2,1)}, bf16[128,2048]{1,0:T(8,128)(2,1)}, u32[]{:S(2)}, u32[]{:S(2)}) collective-permute-start(bf16[128,2048]{1,0:T(8,128)(2,1)} %get-tuple-element.84), channel_id=1, source_target_pairs={{3,2},{2,1},{7,6},{6,5},{11,10},{10,9},{15,14},{14,13},{19,18},{18... | collective-permute-start | bytes 1572872 | tf_op jit(solution)/shard_map/ppermute | solution.py:574
  399.5 32.1 %collective-permute-start.32 = (bf16[256,2048]{1,0:T(8,128)(2,1)S(1)}, bf16[256,2048]{1,0:T(8,128)(2,1)}, u32[]{:S(2)}, u32[]{:S(2)}) collective-permute-start(bf16[256,2048]{1,0:T(8,128)(2,1)S(1)} %copy-done.1), channel_id=1, source_target_pairs={{3,2},{2,1},{1,0},{7,6},{6,5},{5,4},{11,10},{10,9},{9,8},{15,14},{... | collective-permute-start | bytes 3145736 | tf_op jit(solution)/shard_map/ppermute | solution.py:590
  400.8 32.1 %collective-permute-start.34 = (bf16[256,2048]{1,0:T(8,128)(2,1)S(1)}, bf16[256,2048]{1,0:T(8,128)(2,1)}, u32[]{:S(2)}, u32[]{:S(2)}) collective-permute-start(bf16[256,2048]{1,0:T(8,128)(2,1)S(1)} %collective-permute-done.33), channel_id=1, source_target_pairs={{1,2},{2,3},{5,6},{6,7},{9,10},{10,11},{13,14},{14,15},{17,18},{18... | collective-permute-start | bytes 3145736 | tf_op jit(solution)/shard_map/ppermute | solution.py:589
  431.6 56.6 %collective-permute-start.36 = (bf16[256,2048]{1,0:T(8,128)(2,1)}, bf16[256,2048]{1,0:T(8,128)(2,1)}, u32[]{:S(2)}, u32[]{:S(2)}) collective-permute-start(bf16[256,2048]{1,0:T(8,128)(2,1)} %collective-permute-done.32), channel_id=1, source_target_pairs={{2,1},{1,0},{6,5},{5,4},{10,9},{9,8},{14,13},{13,12},{18,17},{17,1... | collective-permute-start | bytes 3145736 | tf_op jit(solution)/shard_map/ppermute | solution.py:590
  432.9 56.8 %collective-permute-start.35 = (bf16[256,2048]{1,0:T(8,128)(2,1)}, bf16[256,2048]{1,0:T(8,128)(2,1)S(1)}, u32[]{:S(2)}, u32[]{:S(2)}) collective-permute-start(bf16[256,2048]{1,0:T(8,128)(2,1)} %collective-permute-done.34), channel_id=1, source_target_pairs={{2,3},{6,7},{10,11},{14,15},{18,19},{22,23},{26,27},{30,31}} | collective-permute-start | bytes 3145736 | tf_op jit(solution)/shard_map/ppermute | solution.py:589
  436.7 38.7 %collective-permute-start.50 = (bf16[128,2048]{1,0:T(8,128)(2,1)S(1)}, bf16[128,2048]{1,0:T(8,128)(2,1)}, u32[]{:S(2)}, u32[]{:S(2)}) collective-permute-start(bf16[128,2048]{1,0:T(8,128)(2,1)S(1)} %copy-done.2), channel_id=1, source_target_pairs={{3,2},{2,1},{1,0},{7,6},{6,5},{5,4},{11,10},{10,9},{9,8},{15,14},{... | collective-permute-start | bytes 1572872 | tf_op jit(solution)/shard_map/ppermute | solution.py:590
  446.2 39.4 %collective-permute-start.56 = (bf16[128,2048]{1,0:T(8,128)(2,1)}, bf16[128,2048]{1,0:T(8,128)(2,1)}, u32[]{:S(2)}, u32[]{:S(2)}) collective-permute-start(bf16[128,2048]{1,0:T(8,128)(2,1)} %shard_map.273), channel_id=1, source_target_pairs={{3,2},{2,1},{1,0},{7,6},{6,5},{5,4},{11,10},{10,9},{9,8},{15,14},{... | collective-permute-start | bytes 1572872 | tf_op jit(solution)/shard_map/ppermute | solution.py:590
  447.5 39.4 %collective-permute-start.53 = (bf16[128,2048]{1,0:T(8,128)(2,1)}, bf16[128,2048]{1,0:T(8,128)(2,1)S(1)}, u32[]{:S(2)}, u32[]{:S(2)}) collective-permute-start(bf16[128,2048]{1,0:T(8,128)(2,1)} %shard_map.273), channel_id=1, source_target_pairs={{0,1},{1,2},{2,3},{4,5},{5,6},{6,7},{8,9},{9,10},{10,11},{12,13},{... | collective-permute-start | bytes 1572872 | tf_op jit(solution)/shard_map/ppermute | solution.py:589
  489.7 44.7 %collective-permute-start.37 = (bf16[256,2048]{1,0:T(8,128)(2,1)}, bf16[256,2048]{1,0:T(8,128)(2,1)}, u32[]{:S(2)}, u32[]{:S(2)}) collective-permute-start(bf16[256,2048]{1,0:T(8,128)(2,1)} %collective-permute-done.36), channel_id=1, source_target_pairs={{1,0},{5,4},{9,8},{13,12},{17,16},{21,20},{25,24},{29,28}} | collective-permute-start | bytes 3145736 | tf_op jit(solution)/shard_map/ppermute | solution.py:590
  (64 other events, 1350.8 us)
Sparse Core Ops, SparseCore 0:
  209.1 77.1 reduce-scatter.2
  289.9 157.3 reduce-scatter.4

commit v2 on v1

--- a/solution.py
+++ b/solution.py
@@ -337,6 +337,32 @@
             out_specs=pl.BlockSpec((each, width), lambda r, w: (w[r], 0)),
         ),
     )(where, *lhs, *rhs)
+
+
+def unpack_kernel(in_ref, *outs):
+    start = 0
+    for i, out in enumerate(outs):
+        width = out.shape[i % 2 == 0]
+        for at in range(0, width, 256):
+            block = in_ref[:, start + at : start + at + 256].astype(F32)
+            if i % 2 == 0:
+                out[:, at : at + 256] = block
+            else:
+                out[at : at + 256, :] = block.T
+        start += width
+
+
+def unpack(grads, widths):
+    rows = grads.shape[0]
+    return call(
+        unpack_kernel,
+        [
+            shape(*((rows, w) if i % 2 == 0 else (w, rows)), dtype=F32)
+            for i, w in enumerate(widths)
+        ],
+        rows * sum(widths),
+        6 * rows * sum(widths),
+    )(grads)
 
 
 def rotary_tables(segments):
@@ -552,27 +578,45 @@
     return up, [(n - 1 - a, n - 1 - b) for a, b in up]
 
 
+def leaving_kernel(at_ref, *refs):
+    refs, outs = refs[:-2], refs[-2:]
+    for i, out in enumerate(outs):
+        rows = refs[i][...].astype(F32)
+        if len(refs) > 2:
+            rows = rows + refs[2 + i][...].astype(F32)
+        out[...] = rows.astype(BF16)
+
+
+def leaving(at, part, tile, got):
+    features = part.shape[1]
+    step = tile // 2
+    own = lambda which: pl.BlockSpec((step, features), lambda i, at: (2 * at[which] + i, 0))
+    here = pl.BlockSpec((step, features), lambda i, at: (i, 0))
+    return call(
+        leaving_kernel,
+        [shape(tile, features)] * 2,
+        2 * tile * features,
+        (4 + 2 * len(got)) * tile * features * 2,
+        grid_spec=pltpu.PrefetchScalarGridSpec(
+            num_scalar_prefetch=1,
+            grid=(2,),
+            in_specs=[own(0), own(1)] + [here] * len(got),
+            out_specs=[here] * 2,
+        ),
+    )(at, part, part, *got)
+
+
 def summed_rows(part):
     n, me = lax.axis_size("mp"), lax.axis_index("mp")
     share = part.shape[0] // n
     tile = share // 2
-    block = lambda j, half: lax.dynamic_slice_in_dim(
-        part, jnp.clip(j, 0, n - 1) * share + half * tile, tile, 0
-    )
-    going = [(block(n - 1 + me, half), block(1 + me - n, half)) for half in (0, 1)]
-    going = lax.optimization_barrier(going)
-    got = [None, None]
+    got = [(), ()]
     for t in range(1, n):
         up, down = neighbours(t, False)
         for half in (0, 1):
-            if t > 1:
-                pair = block(n - t + me, half), block(t + me - n, half)
-                going[half] = lax.optimization_barrier(
-                    tuple(mine + theirs for mine, theirs in zip(pair, got[half]))
-                )
-            got[half] = (
-                lax.ppermute(going[half][0], "mp", up), lax.ppermute(going[half][1], "mp", down)
-            )
+            blocks = jnp.stack([jnp.clip(n - t + me, 0, n - 1), jnp.clip(t + me - n, 0, n - 1)])
+            going = leaving(2 * blocks.astype(jnp.int32) + half, part, tile, got[half])
+            got[half] = (lax.ppermute(going[0], "mp", up), lax.ppermute(going[1], "mp", down))
     return got
 
 
@@ -583,13 +627,13 @@
     for t in range(1, n):
         up, down = neighbours(t, True)
         right, left = [], []
-        if t == n - 1 and late is not None:
-            rights[-1], lefts[-1], late = lax.optimization_barrier((rights[-1], lefts[-1], late))
         for i in range(len(parts)):
             right.append(lax.ppermute(rights[-1][i], "mp", up))
             left.append(lax.ppermute(lefts[-1][i], "mp", down))
         rights.append(right)
         lefts.append(left)
+    if late is not None:
+        room, late = lax.optimization_barrier((room, late))
     for t in range(n):
         for i in range(len(parts)):
             rows = parts[i] if t == 0 else lefts[t][i] + rights[n - t][i]
@@ -678,9 +722,7 @@
     )
     cosine, sine = rotary_tables(segments)
     column = segments.reshape(total, 1)
-    cosine, sine, column, hidden_two = lax.optimization_barrier(
-        (cosine, sine, column, hidden_two)
-    )
+    cosine, sine, column, seed = lax.optimization_barrier((cosine, sine, column, seed))
 
     grad_mixture = mixture_back(seed, dense)
     joint = project(hidden_one, joint_w, bias_j)
@@ -703,18 +745,15 @@
     )
     grads, _ = lax.optimization_barrier((grads, branches))
     grads = lax.psum_scatter(grads, "dp", scatter_dimension=0, tiled=True)
-    cuts = [0]
-    for a in (joint_low, mixture, before_low, activated):
-        cuts.append(cuts[-1] + a.shape[1])
-    piece = lambda i: grads[:, cuts[i] : cuts[i + 1]].astype(F32)
-    weights = (piece(0), piece(1).T, piece(2), piece(3).T)
+    widths = [a.shape[1] for a in (joint_low, mixture, before_low, activated)]
+    weights = unpack(grads, widths)
 
     back = [
         finish(back_kernel, where, half, (inputs, cotangent, marks, gx),
               tuple((a, tile) for a in got), (), (0,))
         for half, got in enumerate(summed_rows(gx))
     ]
-    back, weights = spread_rows(back, gx, weights)
+    back, weights = spread_rows(back, normed, weights)
 
     gains = jnp.sum(gains.reshape(4, 8, features), axis=1)
     gains = summed_over_mp(gains)

time: 574 us -> 592 us (1.031)
  Pallas kernels: 164 us -> 188 us
  waiting for transfers between devices: 210 us -> 222 us
  other arithmetic: 46.9 us -> 35.5 us
  local copies, waits for them, and re-layouts: 26.5 us -> 20 us
    pallas_call x0 -> x7, Pallas kernels: none -> 24 us  [the longest x6 19.1 us: leaving(): call(leaving_kernel, [shape(tile, features)] * 2, 2 * tile * features, (4...]
    ppermute x9, waiting for transfers between devices: 62.9 us -> 79.4 us  [spread_rows(): left.append(lax.ppermute(lefts[-1][i], 'mp', down))]
    ppermute x31, waiting for transfers between devices: 29.3 us -> 14.7 us  [swapped(): return lax.ppermute(a, 'dp', [(i, i ^ bit) for i in range(PIECES)])]
    ppermute x2, waiting for transfers between devices: 8.71 us -> 20.4 us  [summed_over_mp(): values = values + lax.ppermute(values, 'mp', pairs)]
    ppermute x31, starting transfers between devices: 24.7 us -> 35.5 us  [swapped(): return lax.ppermute(a, 'dp', [(i, i ^ bit) for i in range(PIECES)])]
    ppermute x4, waiting for transfers between devices: 47.9 us -> 37.7 us  [crossed_over(): return lax.ppermute(jnp.where(core == 1, from_x, from_y), 'dp', pairs)]
    ppermute x12, starting transfers between devices: 35.2 us -> 28 us  [the longest x6 21.9 us: summed_rows(): lax.ppermute(going[0], 'mp', up)]
    add x3, other arithmetic: 8.46 us -> 1.77 us  [summed_rows(): going = leaving(2 * blocks.astype(jnp.int32) + half, part, tile, got[half])]
  transfers between devices with their start and end apart: 69 -> 69, of which waited for: 20 -> 19; matrix products, arithmetic and copies ran while one was open for 12% -> 8% of each run, Pallas kernels for 26% -> 29%
where the time goes in v2:
time: 592 us; the launch traced here: 590 us
  waiting for transfers between devices  222 us (38%)
  Pallas kernels  188 us (32%)
  starting transfers between devices  110 us (19%)
  other arithmetic  35.5 us (6%)
  local copies, waits for them, and re-layouts  20 us (3%)
  between operations  15 us (3%)
    ppermute x9, waiting for transfers between devices, spread_rows(): left.append(lax.ppermute(lefts[-1][i], 'mp', down))  79.4 us
    ppermute x4, waiting for transfers between devices, crossed_over(): return lax.ppermute(jnp.where(core == 1, from_x, from_y), 'dp', pairs)  37.7 us
    pallas_call x1, Pallas kernels, gradient(): call(gradient_kernel, shape(features, width), 2 * total * features * widt...  35.8 us
    ppermute x31, starting transfers between devices, swapped(): return lax.ppermute(a, 'dp', [(i, i ^ bit) for i in range(PIECES)])  35.5 us
    reduce_scatter x1, waiting for transfers between devices, step(): branches = lax.psum_scatter(branch, 'mp', scatter_dimension=0, tiled=True)  26.8 us
    ppermute x6, waiting for transfers between devices, summed_rows(): lax.ppermute(going[1], 'mp', down)  26.5 us
    pallas_call x1, Pallas kernels, gx_of(): call(gx_kernel, [shape(total, features), shape(32, features, dtype=F32)],...  24.1 us
    ppermute x9, starting transfers between devices, spread_rows(): right.append(lax.ppermute(rights[-1][i], 'mp', up))  23 us
  transfers between devices with their start and end apart: 69, of which 19 were waited for; matrix products, arithmetic and copies ran while one was open for 8% of the time, Pallas kernels for 29%

profile of v2, /device:TPU:0, one launch (start us, length us, event | category | flops | bytes accessed | tf_op | source)
XLA Modules:
  0.0 589.9 jit_solution(17508240969229074401)
XLA Ops:
  10.3 4.7 collective-permute-start.7
  14.9 5.7 collective-permute-start.12
  20.7 5.7 collective-permute-start.14
  35.6 5.1 collective-permute-done.2
  60.1 21.3 %collective-permute-done.16.refs_7_.refs_8_ = bf16[512,256]{1,0:T(8,128)(2,1)S(1)} collective-permute-done((bf16[512,256]{1,0:T(8,128)(2,1)S(1)}, bf16[512,256]{1,0:T(8,128)(2,1)S(1)}, u32[]{:S(2)}, u32[]{:S(2)}) %collective-permute-start.16) | collective-permute-done | bytes 262176 | tf_op jit(solution)/shard_map/ppermute | solution.py:551
  85.4 5.7 collective-permute-start.23
  91.4 16.4 %collective-permute-done.9.refs_7_.refs_10_ = bf16[256,1536]{1,0:T(8,128)(2,1)} collective-permute-done((bf16[256,1536]{1,0:T(8,128)(2,1)S(1)}, bf16[256,1536]{1,0:T(8,128)(2,1)}, u32[]{:S(2)}, u32[]{:S(2)}) %collective-permute-start.9) | collective-permute-done | bytes 786464 | tf_op jit(solution)/shard_map/ppermute | solution.py:551
  110.7 14.1 %shard_map.263 = (bf16[1024,2048]{1,0:T(8,128)(2,1)}, bf16[1024,2048]{1,0:T(8,128)(2,1)}, bf16[1024,2048]{1,0:T(8,128)(2,1)}, bf16[1024,2048]{1,0:T(8,128)(2,1)}, f32[8,2048]{1,0:T(8,128)}) custom-call(s32[9]{0:T(128)} %pad_add_fusion.where_ref, bf16[1024,2048]{1,0:T(8,128)(2,1)} %in_ref.7, bf16[1024,2048]{1,0:T(8,128)(2,1)} %cot_ref.5, ...), custom_call_target="tpu_custom_call" | custom-call | flops 83886080 | bytes 25165824 | tf_op jit(solution)/shard_map/pallas_call | solution.py:96
  132.6 6.2 %shard_map.265.grad_ref = bf16[1024,512]{1,0:T(8,128)(2,1)} custom-call(bf16[1024,2048]{1,0:T(8,128)(2,1)} %get-tuple-element.63.refs_0_.refs_1_.refs_3_, bf16[512,256]{1,0:T(8,128)(2,1)} %refs_2_.1, bf16[512,256]{1,0:T(8,128)(2,1)} %collective-permute-done.11.refs_2_.refs_3_, bf16[512,256]{1,0:T(8,128)(2,1)} %copy-done.16, bf16[512,256]{1,0:T(8,128)(2,1)} %copy-done.31, ...), custom_call_target="tpu_custom_call" | custom-call | flops 2147483648 | bytes 7340032 | tf_op jit(solution)/shard_map/pallas_call | solution.py:175
  138.8 11.8 %shard_map.264.joint_ref = f32[1024,1536]{1,0:T(8,128)} custom-call(bf16[1024,2048]{1,0:T(8,128)(2,1)} %get-tuple-element.60.refs_0_, bf16[256,1536]{1,0:T(8,128)(2,1)} %refs_4_.1, bf16[256,1536]{1,0:T(8,128)(2,1)} %collective-permute-done.4.refs_2_.refs_5_, bf16[256,1536]{1,0:T(8,128)(2,1)} %copy-done.4, ...), custom_call_target="tpu_custom_call" | custom-call | flops 6442450944 | bytes 16777216 | tf_op jit(solution)/shard_map/pallas_call | solution.py:125
  151.8 11.7 %shard_map.266 = (bf16[1024,512]{1,0:T(8,128)(2,1)}, bf16[1024,1536]{1,0:T(8,128)(2,1)}, f32[8,1536]{1,0:T(8,128)}) custom-call(f32[1024,1536]{1,0:T(8,128)} %shard_map.264.joint_ref, bf16[1024,512]{1,0:T(8,128)(2,1)} %shard_map.265.grad_ref, f32[1024,128]{1,0:T(8,128)} %maximum_maximum_fusion.cos_ref, f32[1024,128]{1,0:T(8,128)} %maximum_maximum_fusion.1.sin_ref, ...), custom_call_target="tpu_custom_call" | custom-call | flops 3758096384 | bytes 12582912 | tf_op jit(solution)/shard_map/pallas_call | solution.py:448
  164.5 16.6 %shard_map.267 = (bf16[1024,2048]{1,0:T(8,128)(2,1)}, bf16[1024,2048]{1,0:T(8,128)(2,1)}) custom-call(bf16[1024,2048]{1,0:T(8,128)(2,1)} %get-tuple-element.68.refs_0_.refs_2_, bf16[256,2048]{1,0:T(8,128)(2,1)} %refs_12_.1, bf16[256,2048]{1,0:T(8,128)(2,1)} %collective-permute-done.18.refs_2_.refs_13_, bf16[256,2048]{1,0:T(8,128)(2,1)} %copy-done.3, ...), custom_call_target="tpu_custom_call" | custom-call | flops 8589934592 | bytes 20971520 | tf_op jit(solution)/shard_map/pallas_call | solution.py:151
  183.2 16.8 %shard_map.268 = bf16[1024,2048]{1,0:T(8,128)(2,1)} custom-call(bf16[1024,512]{1,0:T(8,128)(2,1)} %get-tuple-element.67.refs_0_.refs_5_, bf16[1024,2048]{1,0:T(8,128)(2,1)} %get-tuple-element.69.refs_1_.refs_7_, bf16[512,256]{1,0:T(8,128)(2,1)} %refs_2_.1, bf16[512,256]{1,0:T(8,128)(2,1)} %collective-permute-done.11.refs_2_.refs_3_, ...), custom_call_target="tpu_custom_call" | custom-call | flops 10737418240 | bytes 19922944 | tf_op jit(solution)/shard_map/pallas_call | solution.py:259
  200.3 14.3 %shard_map.270 = (bf16[1024,2048]{1,0:T(8,128)(2,1)}, f32[8,2048]{1,0:T(8,128)}) custom-call(bf16[1024,2048]{1,0:T(8,128)(2,1)} %get-tuple-element.63.refs_0_.refs_1_.refs_3_, bf16[2048,256]{1,0:T(8,128)(2,1)} %refs_1_.6, bf16[2048,256]{1,0:T(8,128)(2,1)} %copy-done.26, bf16[2048,256]{1,0:T(8,128)(2,1)} %collective-permute-done.26.refs_12_.refs_3_, ...), custom_call_target="tpu_custom_call" | custom-call | flops 8589934592 | bytes 20971520 | tf_op jit(solution)/shard_map/pallas_call | solution.py:199
  214.6 35.8 %shard_map.271 = bf16[2048,6144]{1,0:T(8,128)(2,1)} custom-call(s32[9]{0:T(128)} %pad_add_fusion.where_ref, bf16[1024,2048]{1,0:T(8,128)(2,1)} %get-tuple-element.60.refs_0_, bf16[1024,2048]{1,0:T(8,128)(2,1)} %get-tuple-element.63.refs_0_.refs_1_.refs_3_, bf16[1024,2048]{1,0:T(8,128)(2,1)} %get-tuple-element.68.refs_0_.refs_2_, ...), custom_call_target="tpu_custom_call" | custom-call | flops 25769803776 | bytes 54525952 | tf_op jit(solution)/shard_map/pallas_call | solution.py:327
  250.3 26.8 %reduce-scatter.3.cloned.1.call-done.got_ref = bf16[256,2048]{1,0:T(8,128)(2,1)} async-done(((bf16[1024,2048]{1,0:T(8,128)(2,1)}), bf16[256,2048]{1,0:T(8,128)(2,1)}) %reduce-scatter.3.cloned.1.call-update) | async-done | bytes 1048592 | tf_op jit(solution)/shard_map/reduce_scatter | solution.py:736
  277.7 24.1 %shard_map.273 = (bf16[1024,2048]{1,0:T(8,128)(2,1)}, f32[32,2048]{1,0:T(8,128)}) custom-call(bf16[1024,1536]{1,0:T(8,128)(2,1)} %get-tuple-element.72.refs_4_.refs_0_, bf16[1024,2048]{1,0:T(8,128)(2,1)} %get-tuple-element.74.refs_6_.refs_1_, bf16[1024,2048]{1,0:T(8,128)(2,1)} %get-tuple-element.80.refs_2_, f32[8,2048]{1,0:T(8,128)} %concatenate.25.vec_ref.refs_3_, ...), custom_call_target="tpu_custom_call" | custom-call | flops 15032385536 | bytes 30408704 | tf_op jit(solution)/shard_map/pallas_call | solution.py:292
  317.9 13.5 %collective-permute-done.62 = f32[4,2048]{1,0:T(4,128)S(1)} collective-permute-done((f32[4,2048]{1,0:T(4,128)S(1)}, f32[4,2048]{1,0:T(4,128)S(1)}, u32[]{:S(2)}, u32[]{:S(2)}) %collective-permute-start.62) | collective-permute-done | bytes 32800 | tf_op jit(solution)/shard_map/ppermute | solution.py:652
  353.3 6.9 %collective-permute-done.63 = f32[4,2048]{1,0:T(4,128)S(1)} collective-permute-done((f32[4,2048]{1,0:T(4,128)S(1)}, f32[4,2048]{1,0:T(4,128)S(1)}, u32[]{:S(2)}, u32[]{:S(2)}) %collective-permute-start.63) | collective-permute-done | bytes 32800 | tf_op jit(solution)/shard_map/ppermute | solution.py:652
  363.0 8.6 %collective-permute-done.46.refs_2_ = bf16[128,2048]{1,0:T(8,128)(2,1)S(1)} collective-permute-done((bf16[128,2048]{1,0:T(8,128)(2,1)}, bf16[128,2048]{1,0:T(8,128)(2,1)S(1)}, u32[]{:S(2)}, u32[]{:S(2)}) %collective-permute-start.46) | collective-permute-done | bytes 524320 | tf_op jit(solution)/shard_map/ppermute | solution.py:619
  375.8 5.9 %collective-permute-start.48 = (bf16[128,2048]{1,0:T(8,128)(2,1)}, bf16[128,2048]{1,0:T(8,128)(2,1)}, u32[]{:S(2)}, u32[]{:S(2)}) collective-permute-start(bf16[128,2048]{1,0:T(8,128)(2,1)} %get-tuple-element.92), channel_id=1, source_target_pairs={{0,1},{1,2},{2,3},{4,5},{5,6},{6,7},{8,9},{9,10},{10,11},{12,13},{... | collective-permute-start | bytes 1572872 | tf_op jit(solution)/shard_map/ppermute | solution.py:619
  387.1 6.2 %collective-permute-start.42 = (bf16[128,2048]{1,0:T(8,128)(2,1)}, bf16[128,2048]{1,0:T(8,128)(2,1)}, u32[]{:S(2)}, u32[]{:S(2)}) collective-permute-start(bf16[128,2048]{1,0:T(8,128)(2,1)} %get-tuple-element.86), channel_id=1, source_target_pairs={{0,1},{1,2},{2,3},{4,5},{5,6},{6,7},{8,9},{9,10},{10,11},{12,13},{... | collective-permute-start | bytes 1572872 | tf_op jit(solution)/shard_map/ppermute | solution.py:619
  404.7 5.5 collective-permute-done.43.above_ref
  411.6 4.7 shard_map.277
  416.2 5.1 collective-permute-start.51
  422.9 21.0 %collective-permute-done.49.above_ref = bf16[128,2048]{1,0:T(8,128)(2,1)S(1)} collective-permute-done((bf16[128,2048]{1,0:T(8,128)(2,1)}, bf16[128,2048]{1,0:T(8,128)(2,1)S(1)}, u32[]{:S(2)}, u32[]{:S(2)}) %collective-permute-start.49) | collective-permute-done | bytes 524320 | tf_op jit(solution)/shard_map/ppermute | solution.py:619
  459.1 4.8 collective-permute-done.55
  465.4 5.0 collective-permute-done.54
  476.7 27.4 %collective-permute-done.58 = bf16[128,2048]{1,0:T(8,128)(2,1)} collective-permute-done((bf16[128,2048]{1,0:T(8,128)(2,1)}, bf16[128,2048]{1,0:T(8,128)(2,1)}, u32[]{:S(2)}, u32[]{:S(2)}) %collective-permute-start.58) | collective-permute-done | bytes 524320 | tf_op jit(solution)/shard_map/ppermute | solution.py:632
  505.5 8.3 %collective-permute-done.59 = bf16[128,2048]{1,0:T(8,128)(2,1)} collective-permute-done((bf16[128,2048]{1,0:T(8,128)(2,1)}, bf16[128,2048]{1,0:T(8,128)(2,1)}, u32[]{:S(2)}, u32[]{:S(2)}) %collective-permute-start.59) | collective-permute-done | bytes 524320 | tf_op jit(solution)/shard_map/ppermute | solution.py:632
  523.2 38.7 %collective-permute-done.37 = bf16[256,2048]{1,0:T(8,128)(2,1)S(1)} collective-permute-done((bf16[256,2048]{1,0:T(8,128)(2,1)}, bf16[256,2048]{1,0:T(8,128)(2,1)S(1)}, u32[]{:S(2)}, u32[]{:S(2)}) %collective-permute-start.37) | collective-permute-done | bytes 1048608 | tf_op jit(solution)/shard_map/ppermute | solution.py:632
  563.3 4.9 shard_map.272
  (283 shorter events, 165.6 us)
Async XLA Ops:
  7.2 269.9 %reduce-scatter.3.cloned.1.call-start = ((), (), s32[]{:S(2)}) async-start(), calls=%async_computation.2 | async-start | bytes 5242880 | tf_op jit(solution)/shard_map/reduce_scatter | solution.py:736
  7.2 48.6 %collective-permute-start.5 = (bf16[256,1536]{1,0:T(8,128)(2,1)}, bf16[256,1536]{1,0:T(8,128)(2,1)S(1)}, u32[]{:S(2)}, u32[]{:S(2)}) collective-permute-start(bf16[256,1536]{1,0:T(8,128)(2,1)} %refs_4_.1), channel_id=1, source_target_pairs={{0,8},{4,12},{8,0},{12,4},{16,24},{20,28},{24,16},{28,20},{1,9},{5... | collective-permute-start | bytes 2359304 | tf_op jit(solution)/shard_map/ppermute | solution.py:545
  10.3 47.6 %collective-permute-start.7 = (bf16[256,1536]{1,0:T(8,128)(2,1)}, bf16[256,1536]{1,0:T(8,128)(2,1)}, u32[]{:S(2)}, u32[]{:S(2)}) collective-permute-start(bf16[256,1536]{1,0:T(8,128)(2,1)} %refs_4_.1), channel_id=1, source_target_pairs={{0,16},{4,20},{8,24},{12,28},{16,0},{20,4},{24,8},{28,12},{1,17},{... | collective-permute-start | bytes 2359304 | tf_op jit(solution)/shard_map/ppermute | solution.py:545
  14.9 36.5 %collective-permute-start.12 = (bf16[512,256]{1,0:T(8,128)(2,1)}, bf16[512,256]{1,0:T(8,128)(2,1)S(1)}, u32[]{:S(2)}, u32[]{:S(2)}) collective-permute-start(bf16[512,256]{1,0:T(8,128)(2,1)} %refs_2_.1), channel_id=1, source_target_pairs={{0,8},{4,12},{8,0},{12,4},{16,24},{20,28},{24,16},{28,20},{1,9},{5... | collective-permute-start | bytes 786440 | tf_op jit(solution)/shard_map/ppermute | solution.py:545
  20.7 31.0 %collective-permute-start.14 = (bf16[512,256]{1,0:T(8,128)(2,1)}, bf16[512,256]{1,0:T(8,128)(2,1)S(1)}, u32[]{:S(2)}, u32[]{:S(2)}) collective-permute-start(bf16[512,256]{1,0:T(8,128)(2,1)} %refs_2_.1), channel_id=1, source_target_pairs={{0,16},{4,20},{8,24},{12,28},{16,0},{20,4},{24,8},{28,12},{1,17},{... | collective-permute-start | bytes 786440 | tf_op jit(solution)/shard_map/ppermute | solution.py:545
  49.5 32.6 %collective-permute-start.19 = (bf16[256,2048]{1,0:T(8,128)(2,1)}, bf16[256,2048]{1,0:T(8,128)(2,1)S(1)}, u32[]{:S(2)}, u32[]{:S(2)}) collective-permute-start(bf16[256,2048]{1,0:T(8,128)(2,1)} %refs_12_.1), channel_id=1, source_target_pairs={{0,8},{4,12},{8,0},{12,4},{16,24},{20,28},{24,16},{28,20},{1,9},{5... | collective-permute-start | bytes 3145736 | tf_op jit(solution)/shard_map/ppermute | solution.py:545
  51.5 31.2 %collective-permute-start.21 = (bf16[256,2048]{1,0:T(8,128)(2,1)}, bf16[256,2048]{1,0:T(8,128)(2,1)}, u32[]{:S(2)}, u32[]{:S(2)}) collective-permute-start(bf16[256,2048]{1,0:T(8,128)(2,1)} %refs_12_.1), channel_id=1, source_target_pairs={{0,16},{4,20},{8,24},{12,28},{16,0},{20,4},{24,8},{28,12},{1,17},{... | collective-permute-start | bytes 3145736 | tf_op jit(solution)/shard_map/ppermute | solution.py:545
  57.8 50.0 %collective-permute-start.26 = (bf16[2048,256]{1,0:T(8,128)(2,1)}, bf16[2048,256]{1,0:T(8,128)(2,1)}, u32[]{:S(2)}, u32[]{:S(2)}) collective-permute-start(bf16[2048,256]{1,0:T(8,128)(2,1)} %refs_1_.6), channel_id=1, source_target_pairs={{0,8},{4,12},{8,0},{12,4},{16,24},{20,28},{24,16},{28,20},{1,9},{5... | collective-permute-start | bytes 3145736 | tf_op jit(solution)/shard_map/ppermute | solution.py:545
  82.7 43.2 %collective-permute-start.28 = (bf16[2048,256]{1,0:T(8,128)(2,1)}, bf16[2048,256]{1,0:T(8,128)(2,1)}, u32[]{:S(2)}, u32[]{:S(2)}) collective-permute-start(bf16[2048,256]{1,0:T(8,128)(2,1)} %refs_1_.6), channel_id=1, source_target_pairs={{0,16},{4,20},{8,24},{12,28},{16,0},{20,4},{24,8},{28,12},{1,17},{... | collective-permute-start | bytes 3145736 | tf_op jit(solution)/shard_map/ppermute | solution.py:545
  85.4 43.9 %collective-permute-start.23 = (bf16[256,2048]{1,0:T(8,128)(2,1)}, bf16[256,2048]{1,0:T(8,128)(2,1)}, u32[]{:S(2)}, u32[]{:S(2)}) collective-permute-start(bf16[256,2048]{1,0:T(8,128)(2,1)} %broadcast_select_fusion.1), channel_id=1, source_target_pairs={{0,8},{4,20},{8,0},{12,28},{16,24},{20,4},{24,16},{28,12},{1,9},{5... | collective-permute-start | bytes 3145736 | tf_op jit(solution)/shard_map/ppermute | solution.py:551
  91.2 37.0 %collective-permute-start.4 = (bf16[256,1536]{1,0:T(8,128)(2,1)}, bf16[256,1536]{1,0:T(8,128)(2,1)}, u32[]{:S(2)}, u32[]{:S(2)}) collective-permute-start(bf16[256,1536]{1,0:T(8,128)(2,1)} %refs_4_.1), channel_id=1, source_target_pairs={{0,4},{4,0},{8,12},{12,8},{16,20},{20,16},{24,28},{28,24},{1,5},{5... | collective-permute-start | bytes 2359304 | tf_op jit(solution)/shard_map/ppermute | solution.py:545
  200.0 363.3 %reduce-scatter.5.cloned.1.call-start = ((), (), s32[]{:S(2)}) async-start(), calls=%async_computation.3 | async-start | bytes 28311552 | tf_op jit(solution)/shard_map/reduce_scatter | solution.py:747
  304.8 31.1 %collective-permute-start.44 = (bf16[128,2048]{1,0:T(8,128)(2,1)}, bf16[128,2048]{1,0:T(8,128)(2,1)S(1)}, u32[]{:S(2)}, u32[]{:S(2)}) collective-permute-start(bf16[128,2048]{1,0:T(8,128)(2,1)} %get-tuple-element.88), channel_id=1, source_target_pairs={{0,1},{4,5},{8,9},{12,13},{16,17},{20,21},{24,25},{28,29}} | collective-permute-start | bytes 1572872 | tf_op jit(solution)/shard_map/ppermute | solution.py:619
  312.1 33.4 %collective-permute-start.38 = (bf16[128,2048]{1,0:T(8,128)(2,1)}, bf16[128,2048]{1,0:T(8,128)(2,1)S(1)}, u32[]{:S(2)}, u32[]{:S(2)}) collective-permute-start(bf16[128,2048]{1,0:T(8,128)(2,1)} %get-tuple-element.82), channel_id=1, source_target_pairs={{0,1},{4,5},{8,9},{12,13},{16,17},{20,21},{24,25},{28,29}} | collective-permute-start | bytes 1572872 | tf_op jit(solution)/shard_map/ppermute | solution.py:619
  313.5 33.5 %collective-permute-start.39 = (bf16[128,2048]{1,0:T(8,128)(2,1)}, bf16[128,2048]{1,0:T(8,128)(2,1)S(1)}, u32[]{:S(2)}, u32[]{:S(2)}) collective-permute-start(bf16[128,2048]{1,0:T(8,128)(2,1)} %get-tuple-element.83), channel_id=1, source_target_pairs={{3,2},{7,6},{11,10},{15,14},{19,18},{23,22},{27,26},{31,30}} | collective-permute-start | bytes 1572872 | tf_op jit(solution)/shard_map/ppermute | solution.py:619
  331.4 68.6 %collective-permute-start.33 = (bf16[256,2048]{1,0:T(8,128)(2,1)}, bf16[256,2048]{1,0:T(8,128)(2,1)S(1)}, u32[]{:S(2)}, u32[]{:S(2)}) collective-permute-start(bf16[256,2048]{1,0:T(8,128)(2,1)} %shard_map.269), channel_id=1, source_target_pairs={{0,1},{1,2},{2,3},{4,5},{5,6},{6,7},{8,9},{9,10},{10,11},{12,13},{... | collective-permute-start | bytes 3145736 | tf_op jit(solution)/shard_map/ppermute | solution.py:631
  351.0 31.8 %collective-permute-start.40 = (bf16[128,2048]{1,0:T(8,128)(2,1)}, bf16[128,2048]{1,0:T(8,128)(2,1)S(1)}, u32[]{:S(2)}, u32[]{:S(2)}) collective-permute-start(bf16[128,2048]{1,0:T(8,128)(2,1)} %get-tuple-element.84), channel_id=1, source_target_pairs={{0,1},{1,2},{4,5},{5,6},{8,9},{9,10},{12,13},{13,14},{16,17},{17,1... | collective-permute-start | bytes 1572872 | tf_op jit(solution)/shard_map/ppermute | solution.py:619
  375.8 45.5 %collective-permute-start.48 = (bf16[128,2048]{1,0:T(8,128)(2,1)}, bf16[128,2048]{1,0:T(8,128)(2,1)}, u32[]{:S(2)}, u32[]{:S(2)}) collective-permute-start(bf16[128,2048]{1,0:T(8,128)(2,1)} %get-tuple-element.92), channel_id=1, source_target_pairs={{0,1},{1,2},{2,3},{4,5},{5,6},{6,7},{8,9},{9,10},{10,11},{12,13},{... | collective-permute-start | bytes 1572872 | tf_op jit(solution)/shard_map/ppermute | solution.py:619
  398.8 57.4 %collective-permute-start.32 = (bf16[256,2048]{1,0:T(8,128)(2,1)S(1)}, bf16[256,2048]{1,0:T(8,128)(2,1)S(1)}, u32[]{:S(2)}, u32[]{:S(2)}) collective-permute-start(bf16[256,2048]{1,0:T(8,128)(2,1)S(1)} %copy-done), channel_id=1, source_target_pairs={{3,2},{2,1},{1,0},{7,6},{6,5},{5,4},{11,10},{10,9},{9,8},{15,14},{... | collective-permute-start | bytes 3145736 | tf_op jit(solution)/shard_map/ppermute | solution.py:632
  400.1 57.4 %collective-permute-start.34 = (bf16[256,2048]{1,0:T(8,128)(2,1)S(1)}, bf16[256,2048]{1,0:T(8,128)(2,1)}, u32[]{:S(2)}, u32[]{:S(2)}) collective-permute-start(bf16[256,2048]{1,0:T(8,128)(2,1)S(1)} %collective-permute-done.33), channel_id=1, source_target_pairs={{1,2},{2,3},{5,6},{6,7},{9,10},{10,11},{13,14},{14,15},{17,18},{18... | collective-permute-start | bytes 3145736 | tf_op jit(solution)/shard_map/ppermute | solution.py:631
  410.3 33.6 %collective-permute-start.49 = (bf16[128,2048]{1,0:T(8,128)(2,1)}, bf16[128,2048]{1,0:T(8,128)(2,1)S(1)}, u32[]{:S(2)}, u32[]{:S(2)}) collective-permute-start(bf16[128,2048]{1,0:T(8,128)(2,1)} %get-tuple-element.93), channel_id=1, source_target_pairs={{3,2},{2,1},{1,0},{7,6},{6,5},{5,4},{11,10},{10,9},{9,8},{15,14},{... | collective-permute-start | bytes 1572872 | tf_op jit(solution)/shard_map/ppermute | solution.py:619
  416.2 37.1 %collective-permute-start.51 = (bf16[128,2048]{1,0:T(8,128)(2,1)}, bf16[128,2048]{1,0:T(8,128)(2,1)}, u32[]{:S(2)}, u32[]{:S(2)}) collective-permute-start(bf16[128,2048]{1,0:T(8,128)(2,1)} %shard_map.277), channel_id=1, source_target_pairs={{0,1},{1,2},{2,3},{4,5},{5,6},{6,7},{8,9},{9,10},{10,11},{12,13},{... | collective-permute-start | bytes 1572872 | tf_op jit(solution)/shard_map/ppermute | solution.py:631
  421.3 33.4 %collective-permute-start.50 = (bf16[128,2048]{1,0:T(8,128)(2,1)}, bf16[128,2048]{1,0:T(8,128)(2,1)S(1)}, u32[]{:S(2)}, u32[]{:S(2)}) collective-permute-start(bf16[128,2048]{1,0:T(8,128)(2,1)} %shard_map.277), channel_id=1, source_target_pairs={{3,2},{2,1},{1,0},{7,6},{6,5},{5,4},{11,10},{10,9},{9,8},{15,14},{... | collective-permute-start | bytes 1572872 | tf_op jit(solution)/shard_map/ppermute | solution.py:632
  456.2 58.9 %collective-permute-start.36 = (bf16[256,2048]{1,0:T(8,128)(2,1)S(1)}, bf16[256,2048]{1,0:T(8,128)(2,1)}, u32[]{:S(2)}, u32[]{:S(2)}) collective-permute-start(bf16[256,2048]{1,0:T(8,128)(2,1)S(1)} %collective-permute-done.32), channel_id=1, source_target_pairs={{2,1},{1,0},{6,5},{5,4},{10,9},{9,8},{14,13},{13,12},{18,17},{17,1... | collective-permute-start | bytes 3145736 | tf_op jit(solution)/shard_map/ppermute | solution.py:632
  457.5 58.9 %collective-permute-start.35 = (bf16[256,2048]{1,0:T(8,128)(2,1)}, bf16[256,2048]{1,0:T(8,128)(2,1)}, u32[]{:S(2)}, u32[]{:S(2)}) collective-permute-start(bf16[256,2048]{1,0:T(8,128)(2,1)} %collective-permute-done.34), channel_id=1, source_target_pairs={{2,3},{6,7},{10,11},{14,15},{18,19},{22,23},{26,27},{30,31}} | collective-permute-start | bytes 3145736 | tf_op jit(solution)/shard_map/ppermute | solution.py:631
  470.4 33.7 %collective-permute-start.58 = (bf16[128,2048]{1,0:T(8,128)(2,1)}, bf16[128,2048]{1,0:T(8,128)(2,1)}, u32[]{:S(2)}, u32[]{:S(2)}) collective-permute-start(bf16[128,2048]{1,0:T(8,128)(2,1)} %copy-done.13), channel_id=1, source_target_pairs={{2,1},{1,0},{6,5},{5,4},{10,9},{9,8},{14,13},{13,12},{18,17},{17,1... | collective-permute-start | bytes 1572872 | tf_op jit(solution)/shard_map/ppermute | solution.py:632
  471.7 42.1 %collective-permute-start.59 = (bf16[128,2048]{1,0:T(8,128)(2,1)}, bf16[128,2048]{1,0:T(8,128)(2,1)}, u32[]{:S(2)}, u32[]{:S(2)}) collective-permute-start(bf16[128,2048]{1,0:T(8,128)(2,1)} %collective-permute-done.54), channel_id=1, source_target_pairs={{2,1},{1,0},{6,5},{5,4},{10,9},{9,8},{14,13},{13,12},{18,17},{17,1... | collective-permute-start | bytes 1572872 | tf_op jit(solution)/shard_map/ppermute | solution.py:632
  475.2 94.6 %collective-permute-start.53 = (bf16[128,2048]{1,0:T(8,128)(2,1)}, bf16[128,2048]{1,0:T(8,128)(2,1)}, u32[]{:S(2)}, u32[]{:S(2)}) collective-permute-start(bf16[128,2048]{1,0:T(8,128)(2,1)} %collective-permute-done.52), channel_id=1, source_target_pairs={{2,3},{6,7},{10,11},{14,15},{18,19},{22,23},{26,27},{30,31}} | collective-permute-start | bytes 1572872 | tf_op jit(solution)/shard_map/ppermute | solution.py:631
  504.1 67.8 %collective-permute-start.57 = (bf16[128,2048]{1,0:T(8,128)(2,1)}, bf16[128,2048]{1,0:T(8,128)(2,1)}, u32[]{:S(2)}, u32[]{:S(2)}) collective-permute-start(bf16[128,2048]{1,0:T(8,128)(2,1)} %collective-permute-done.56), channel_id=1, source_target_pairs={{2,3},{6,7},{10,11},{14,15},{18,19},{22,23},{26,27},{30,31}} | collective-permute-start | bytes 1572872 | tf_op jit(solution)/shard_map/ppermute | solution.py:631
  513.8 64.4 %collective-permute-start.60 = (bf16[128,2048]{1,0:T(8,128)(2,1)}, bf16[128,2048]{1,0:T(8,128)(2,1)}, u32[]{:S(2)}, u32[]{:S(2)}) collective-permute-start(bf16[128,2048]{1,0:T(8,128)(2,1)} %collective-permute-done.58), channel_id=1, source_target_pairs={{1,0},{5,4},{9,8},{13,12},{17,16},{21,20},{25,24},{29,28}} | collective-permute-start | bytes 1572872 | tf_op jit(solution)/shard_map/ppermute | solution.py:632
  515.1 65.3 %collective-permute-start.61 = (bf16[128,2048]{1,0:T(8,128)(2,1)}, bf16[128,2048]{1,0:T(8,128)(2,1)}, u32[]{:S(2)}, u32[]{:S(2)}) collective-permute-start(bf16[128,2048]{1,0:T(8,128)(2,1)} %collective-permute-done.59), channel_id=1, source_target_pairs={{1,0},{5,4},{9,8},{13,12},{17,16},{21,20},{25,24},{29,28}} | collective-permute-start | bytes 1572872 | tf_op jit(solution)/shard_map/ppermute | solution.py:632
  516.4 45.6 %collective-permute-start.37 = (bf16[256,2048]{1,0:T(8,128)(2,1)}, bf16[256,2048]{1,0:T(8,128)(2,1)S(1)}, u32[]{:S(2)}, u32[]{:S(2)}) collective-permute-start(bf16[256,2048]{1,0:T(8,128)(2,1)} %collective-permute-done.36), channel_id=1, source_target_pairs={{1,0},{5,4},{9,8},{13,12},{17,16},{21,20},{25,24},{29,28}} | collective-permute-start | bytes 3145736 | tf_op jit(solution)/shard_map/ppermute | solution.py:632
  (71 other events, 1260.1 us)
Sparse Core Ops, SparseCore 0:
  200.1 76.8 reduce-scatter.2
  280.7 157.0 reduce-scatter.4

commit v3 on v2

--- a/solution.py
+++ b/solution.py
@@ -615,7 +615,8 @@
         up, down = neighbours(t, False)
         for half in (0, 1):
             blocks = jnp.stack([jnp.clip(n - t + me, 0, n - 1), jnp.clip(t + me - n, 0, n - 1)])
-            going = leaving(2 * blocks.astype(jnp.int32) + half, part, tile, got[half])
+            at = 2 * blocks.astype(jnp.int32) + half
+            going = leaving(at, part, tile, got[half])
             got[half] = (lax.ppermute(going[0], "mp", up), lax.ppermute(going[1], "mp", down))
     return got
 
@@ -632,9 +633,9 @@
             left.append(lax.ppermute(lefts[-1][i], "mp", down))
         rights.append(right)
         lefts.append(left)
-    if late is not None:
-        room, late = lax.optimization_barrier((room, late))
-    for t in range(n):
+    for t in [0] + list(range(2, n - 1)) + ([1, n - 1] if n > 2 else [1]):
+        if t == 1 and late is not None:
+            room, late = lax.optimization_barrier((room, late))
         for i in range(len(parts)):
             rows = parts[i] if t == 0 else lefts[t][i] + rights[n - t][i]
             at = (lax.rem(me + t, n) * len(parts) + i) * tile

time: 592 us -> 557 us (0.941)
  waiting for transfers between devices: 222 us -> 186 us
    ppermute x6, waiting for transfers between devices: 26.5 us -> 0.02 us  [summed_rows(): lax.ppermute(going[1], 'mp', down)]
    ppermute x9, waiting for transfers between devices: 79.4 us -> 65.9 us  [spread_rows(): left.append(lax.ppermute(lefts[-1][i], 'mp', down))]
    ppermute x2, waiting for transfers between devices: 20.4 us -> 10.2 us  [summed_over_mp(): values = values + lax.ppermute(values, 'mp', pairs)]
    ppermute x31, waiting for transfers between devices: 14.7 us -> 24.7 us  [swapped(): return lax.ppermute(a, 'dp', [(i, i ^ bit) for i in range(PIECES)])]
    ppermute x9, waiting for transfers between devices: 4.81 us -> 12.6 us  [spread_rows(): right.append(lax.ppermute(rights[-1][i], 'mp', up))]
  transfers between devices with their start and end apart: 69 -> 69, of which waited for: 19 -> 21; matrix products, arithmetic and copies ran while one was open for 8% -> 7% of each run, Pallas kernels for 29% -> 31%
where the time goes in v3:
time: 557 us; the launch traced here: 549 us
  Pallas kernels  188 us (34%)
  waiting for transfers between devices  186 us (33%)
  starting transfers between devices  109 us (20%)
  other arithmetic  29.9 us (5%)
  local copies, waits for them, and re-layouts  21 us (4%)
  between operations  15.1 us (3%)
    ppermute x9, waiting for transfers between devices, spread_rows(): left.append(lax.ppermute(lefts[-1][i], 'mp', down))  65.9 us
    ppermute x4, waiting for transfers between devices, crossed_over(): return lax.ppermute(jnp.where(core == 1, from_x, from_y), 'dp', pairs)  39.8 us
    pallas_call x1, Pallas kernels, gradient(): call(gradient_kernel, shape(features, width), 2 * total * features * widt...  35.7 us
    ppermute x31, starting transfers between devices, swapped(): return lax.ppermute(a, 'dp', [(i, i ^ bit) for i in range(PIECES)])  35.3 us
    reduce_scatter x1, waiting for transfers between devices, step(): branches = lax.psum_scatter(branch, 'mp', scatter_dimension=0, tiled=True)  26.7 us
    ppermute x31, waiting for transfers between devices, swapped(): return lax.ppermute(a, 'dp', [(i, i ^ bit) for i in range(PIECES)])  24.7 us
    pallas_call x1, Pallas kernels, gx_of(): call(gx_kernel, [shape(total, features), shape(32, features, dtype=F32)],...  24.2 us
    ppermute x9, starting transfers between devices, spread_rows(): right.append(lax.ppermute(rights[-1][i], 'mp', up))  21.3 us
  transfers between devices with their start and end apart: 69, of which 21 were waited for; matrix products, arithmetic and copies ran while one was open for 7% of the time, Pallas kernels for 31%

profile of v3, /device:TPU:0, one launch (start us, length us, event | category | flops | bytes accessed | tf_op | source)
XLA Modules:
  0.0 549.1 jit_solution(17640382539220163403)
XLA Ops:
  20.3 13.5 %collective-permute-done.1 = bf16[2,8,256]{2,1,0:T(8,128)(2,1)S(1)} collective-permute-done((bf16[2,8,256]{2,1,0:T(8,128)(2,1)S(1)}, bf16[2,8,256]{2,1,0:T(8,128)(2,1)S(1)}, u32[]{:S(2)}, u32[]{:S(2)}) %collective-permute-start.1) | collective-permute-done | bytes 8224 | tf_op jit(solution)/shard_map/ppermute | solution.py:545
  37.5 5.9 %collective-permute-start.3 = (bf16[2,8,256]{2,1,0:T(8,128)(2,1)S(1)}, bf16[2,8,256]{2,1,0:T(8,128)(2,1)S(1)}, u32[]{:S(2)}, u32[]{:S(2)}) collective-permute-start(bf16[2,8,256]{2,1,0:T(8,128)(2,1)S(1)} %pad_maximum_fusion), channel_id=1, source_target_pairs={{0,24},{4,28},{8,16},{12,20},{16,8},{20,12},{24,0},{28,4},{1,25},{... | collective-permute-start | bytes 24584 | tf_op jit(solution)/shard_map/ppermute | solution.py:545
  43.3 4.4 collective-permute-done.3
  63.6 20.0 %collective-permute-done.16.refs_7_.refs_8_ = bf16[512,256]{1,0:T(8,128)(2,1)S(1)} collective-permute-done((bf16[512,256]{1,0:T(8,128)(2,1)S(1)}, bf16[512,256]{1,0:T(8,128)(2,1)S(1)}, u32[]{:S(2)}, u32[]{:S(2)}) %collective-permute-start.16) | collective-permute-done | bytes 262176 | tf_op jit(solution)/shard_map/ppermute | solution.py:551
  85.6 5.9 %collective-permute-start.23 = (bf16[256,2048]{1,0:T(8,128)(2,1)}, bf16[256,2048]{1,0:T(8,128)(2,1)}, u32[]{:S(2)}, u32[]{:S(2)}) collective-permute-start(bf16[256,2048]{1,0:T(8,128)(2,1)} %broadcast_select_fusion.1), channel_id=1, source_target_pairs={{0,8},{4,20},{8,0},{12,28},{16,24},{20,4},{24,16},{28,12},{1,9},{5... | collective-permute-start | bytes 3145736 | tf_op jit(solution)/shard_map/ppermute | solution.py:551
  91.9 17.9 %collective-permute-done.9.refs_7_.refs_10_ = bf16[256,1536]{1,0:T(8,128)(2,1)} collective-permute-done((bf16[256,1536]{1,0:T(8,128)(2,1)S(1)}, bf16[256,1536]{1,0:T(8,128)(2,1)}, u32[]{:S(2)}, u32[]{:S(2)}) %collective-permute-start.9) | collective-permute-done | bytes 786464 | tf_op jit(solution)/shard_map/ppermute | solution.py:551
  121.4 14.1 %shard_map.263 = (bf16[1024,2048]{1,0:T(8,128)(2,1)}, bf16[1024,2048]{1,0:T(8,128)(2,1)}, bf16[1024,2048]{1,0:T(8,128)(2,1)}, bf16[1024,2048]{1,0:T(8,128)(2,1)}, f32[8,2048]{1,0:T(8,128)}) custom-call(s32[9]{0:T(128)} %pad_add_fusion.where_ref, bf16[1024,2048]{1,0:T(8,128)(2,1)} %in_ref.7, bf16[1024,2048]{1,0:T(8,128)(2,1)} %cot_ref.5, ...), custom_call_target="tpu_custom_call" | custom-call | flops 83886080 | bytes 25165824 | tf_op jit(solution)/shard_map/pallas_call | solution.py:96
  141.1 6.2 %shard_map.265.grad_ref = bf16[1024,512]{1,0:T(8,128)(2,1)} custom-call(bf16[1024,2048]{1,0:T(8,128)(2,1)} %get-tuple-element.63.refs_0_.refs_1_.refs_3_, bf16[512,256]{1,0:T(8,128)(2,1)} %refs_2_.1, bf16[512,256]{1,0:T(8,128)(2,1)} %collective-permute-done.11.refs_2_.refs_3_, bf16[512,256]{1,0:T(8,128)(2,1)} %copy-done.18, bf16[512,256]{1,0:T(8,128)(2,1)} %copy-done.32, ...), custom_call_target="tpu_custom_call" | custom-call | flops 2147483648 | bytes 7340032 | tf_op jit(solution)/shard_map/pallas_call | solution.py:175
  147.4 11.8 %shard_map.264.joint_ref = f32[1024,1536]{1,0:T(8,128)} custom-call(bf16[1024,2048]{1,0:T(8,128)(2,1)} %get-tuple-element.60.refs_0_, bf16[256,1536]{1,0:T(8,128)(2,1)} %refs_4_.1, bf16[256,1536]{1,0:T(8,128)(2,1)} %collective-permute-done.4.refs_2_.refs_5_, bf16[256,1536]{1,0:T(8,128)(2,1)} %collective-permute-done.5.refs_3_.refs_6_, ...), custom_call_target="tpu_custom_call" | custom-call | flops 6442450944 | bytes 16777216 | tf_op jit(solution)/shard_map/pallas_call | solution.py:125
  160.3 11.7 %shard_map.266 = (bf16[1024,512]{1,0:T(8,128)(2,1)}, bf16[1024,1536]{1,0:T(8,128)(2,1)}, f32[8,1536]{1,0:T(8,128)}) custom-call(f32[1024,1536]{1,0:T(8,128)} %shard_map.264.joint_ref, bf16[1024,512]{1,0:T(8,128)(2,1)} %shard_map.265.grad_ref, f32[1024,128]{1,0:T(8,128)} %maximum_maximum_fusion.cos_ref, f32[1024,128]{1,0:T(8,128)} %maximum_maximum_fusion.1.sin_ref, ...), custom_call_target="tpu_custom_call" | custom-call | flops 3758096384 | bytes 12582912 | tf_op jit(solution)/shard_map/pallas_call | solution.py:448
  173.0 16.6 %shard_map.267 = (bf16[1024,2048]{1,0:T(8,128)(2,1)}, bf16[1024,2048]{1,0:T(8,128)(2,1)}) custom-call(bf16[1024,2048]{1,0:T(8,128)(2,1)} %get-tuple-element.68.refs_0_.refs_2_, bf16[256,2048]{1,0:T(8,128)(2,1)} %refs_12_.1, bf16[256,2048]{1,0:T(8,128)(2,1)} %collective-permute-done.18.refs_2_.refs_13_, bf16[256,2048]{1,0:T(8,128)(2,1)} %copy-done.2, ...), custom_call_target="tpu_custom_call" | custom-call | flops 8589934592 | bytes 20971520 | tf_op jit(solution)/shard_map/pallas_call | solution.py:151
  191.7 16.8 %shard_map.268 = bf16[1024,2048]{1,0:T(8,128)(2,1)} custom-call(bf16[1024,512]{1,0:T(8,128)(2,1)} %get-tuple-element.67.refs_0_.refs_5_, bf16[1024,2048]{1,0:T(8,128)(2,1)} %get-tuple-element.69.refs_1_.refs_7_, bf16[512,256]{1,0:T(8,128)(2,1)} %refs_2_.1, bf16[512,256]{1,0:T(8,128)(2,1)} %collective-permute-done.11.refs_2_.refs_3_, ...), custom_call_target="tpu_custom_call" | custom-call | flops 10737418240 | bytes 19922944 | tf_op jit(solution)/shard_map/pallas_call | solution.py:259
  208.8 14.2 %shard_map.270 = (bf16[1024,2048]{1,0:T(8,128)(2,1)}, f32[8,2048]{1,0:T(8,128)}) custom-call(bf16[1024,2048]{1,0:T(8,128)(2,1)} %get-tuple-element.63.refs_0_.refs_1_.refs_3_, bf16[2048,256]{1,0:T(8,128)(2,1)} %refs_1_.6, bf16[2048,256]{1,0:T(8,128)(2,1)} %copy-done.27, bf16[2048,256]{1,0:T(8,128)(2,1)} %collective-permute-done.26.refs_12_.refs_3_, ...), custom_call_target="tpu_custom_call" | custom-call | flops 8589934592 | bytes 20971520 | tf_op jit(solution)/shard_map/pallas_call | solution.py:199
  223.0 35.7 %shard_map.280 = bf16[2048,6144]{1,0:T(8,128)(2,1)} custom-call(s32[9]{0:T(128)} %pad_add_fusion.where_ref, bf16[1024,2048]{1,0:T(8,128)(2,1)} %get-tuple-element.60.refs_0_, bf16[1024,2048]{1,0:T(8,128)(2,1)} %get-tuple-element.63.refs_0_.refs_1_.refs_3_, bf16[1024,2048]{1,0:T(8,128)(2,1)} %get-tuple-element.68.refs_0_.refs_2_, ...), custom_call_target="tpu_custom_call" | custom-call | flops 25769803776 | bytes 54525952 | tf_op jit(solution)/shard_map/pallas_call | solution.py:327
  258.8 26.7 %reduce-scatter.3.cloned.1.call-done.got_ref = bf16[256,2048]{1,0:T(8,128)(2,1)} async-done(((bf16[1024,2048]{1,0:T(8,128)(2,1)}), bf16[256,2048]{1,0:T(8,128)(2,1)}) %reduce-scatter.3.cloned.1.call-update) | async-done | bytes 1048592 | tf_op jit(solution)/shard_map/reduce_scatter | solution.py:737
  286.1 24.2 %shard_map.271 = (bf16[1024,2048]{1,0:T(8,128)(2,1)}, f32[32,2048]{1,0:T(8,128)}) custom-call(bf16[1024,1536]{1,0:T(8,128)(2,1)} %get-tuple-element.72.refs_0_.refs_4_, bf16[1024,2048]{1,0:T(8,128)(2,1)} %get-tuple-element.74.refs_1_.refs_6_, bf16[1024,2048]{1,0:T(8,128)(2,1)} %get-tuple-element.71.refs_2_, f32[8,2048]{1,0:T(8,128)} %concatenate.25.vec_ref.refs_3_, ...), custom_call_target="tpu_custom_call" | custom-call | flops 15032385536 | bytes 30408704 | tf_op jit(solution)/shard_map/pallas_call | solution.py:292
  322.9 6.3 %collective-permute-done.38.refs_2_ = bf16[128,2048]{1,0:T(8,128)(2,1)S(1)} collective-permute-done((bf16[128,2048]{1,0:T(8,128)(2,1)}, bf16[128,2048]{1,0:T(8,128)(2,1)S(1)}, u32[]{:S(2)}, u32[]{:S(2)}) %collective-permute-start.38) | collective-permute-done | bytes 524320 | tf_op jit(solution)/shard_map/ppermute | solution.py:620
  334.0 4.3 collective-permute-start.40
  344.7 4.5 collective-permute-start.46
  363.6 4.6 collective-permute-start.63
  368.2 8.8 %collective-permute-done.63 = f32[4,2048]{1,0:T(4,128)S(1)} collective-permute-done((f32[4,2048]{1,0:T(4,128)S(1)}, f32[4,2048]{1,0:T(4,128)S(1)}, u32[]{:S(2)}, u32[]{:S(2)}) %collective-permute-start.63) | collective-permute-done | bytes 32800 | tf_op jit(solution)/shard_map/ppermute | solution.py:653
  389.7 4.5 shard_map.275
  395.4 5.9 %collective-permute-start.52 = (bf16[128,2048]{1,0:T(8,128)(2,1)}, bf16[128,2048]{1,0:T(8,128)(2,1)}, u32[]{:S(2)}, u32[]{:S(2)}) collective-permute-start(bf16[128,2048]{1,0:T(8,128)(2,1)} %shard_map.275), channel_id=1, source_target_pairs={{0,1},{1,2},{2,3},{4,5},{5,6},{6,7},{8,9},{9,10},{10,11},{12,13},{... | collective-permute-start | bytes 1572872 | tf_op jit(solution)/shard_map/ppermute | solution.py:632
  409.9 4.4 shard_map.279
  416.9 4.6 collective-permute-start.56
  427.9 7.7 %collective-permute-done.34 = bf16[256,2048]{1,0:T(8,128)(2,1)S(1)} collective-permute-done((bf16[256,2048]{1,0:T(8,128)(2,1)}, bf16[256,2048]{1,0:T(8,128)(2,1)S(1)}, u32[]{:S(2)}, u32[]{:S(2)}) %collective-permute-start.34) | collective-permute-done | bytes 1048608 | tf_op jit(solution)/shard_map/ppermute | solution.py:632
  438.4 4.9 collective-permute-done.56
  449.4 11.4 %collective-permute-done.32 = bf16[256,2048]{1,0:T(8,128)(2,1)S(1)} collective-permute-done((bf16[256,2048]{1,0:T(8,128)(2,1)S(1)}, bf16[256,2048]{1,0:T(8,128)(2,1)S(1)}, u32[]{:S(2)}, u32[]{:S(2)}) %collective-permute-start.32) | collective-permute-done | bytes 1048608 | tf_op jit(solution)/shard_map/ppermute | solution.py:633
  464.2 7.8 %collective-permute-done.55 = bf16[128,2048]{1,0:T(8,128)(2,1)S(1)} collective-permute-done((bf16[128,2048]{1,0:T(8,128)(2,1)S(1)}, bf16[128,2048]{1,0:T(8,128)(2,1)S(1)}, u32[]{:S(2)}, u32[]{:S(2)}) %collective-permute-start.55) | collective-permute-done | bytes 524320 | tf_op jit(solution)/shard_map/ppermute | solution.py:633
  478.6 15.9 %collective-permute-done.33 = bf16[256,2048]{1,0:T(8,128)(2,1)S(1)} collective-permute-done((bf16[256,2048]{1,0:T(8,128)(2,1)S(1)}, bf16[256,2048]{1,0:T(8,128)(2,1)S(1)}, u32[]{:S(2)}, u32[]{:S(2)}) %collective-permute-start.33) | collective-permute-done | bytes 1048608 | tf_op jit(solution)/shard_map/ppermute | solution.py:633
  499.8 28.4 %collective-permute-done.37 = bf16[256,2048]{1,0:T(8,128)(2,1)S(1)} collective-permute-done((bf16[256,2048]{1,0:T(8,128)(2,1)S(1)}, bf16[256,2048]{1,0:T(8,128)(2,1)S(1)}, u32[]{:S(2)}, u32[]{:S(2)}) %collective-permute-start.37) | collective-permute-done | bytes 1048608 | tf_op jit(solution)/shard_map/ppermute | solution.py:633
  529.6 4.9 shard_map.281
  (285 shorter events, 159.3 us)
Async XLA Ops:
  7.2 278.3 %reduce-scatter.3.cloned.1.call-start = ((), (), s32[]{:S(2)}) async-start(), calls=%async_computation.2 | async-start | bytes 5242880 | tf_op jit(solution)/shard_map/reduce_scatter | solution.py:737
  7.2 51.4 %collective-permute-start.5 = (bf16[256,1536]{1,0:T(8,128)(2,1)}, bf16[256,1536]{1,0:T(8,128)(2,1)}, u32[]{:S(2)}, u32[]{:S(2)}) collective-permute-start(bf16[256,1536]{1,0:T(8,128)(2,1)} %refs_4_.1), channel_id=1, source_target_pairs={{0,8},{4,12},{8,0},{12,4},{16,24},{20,28},{24,16},{28,20},{1,9},{5... | collective-permute-start | bytes 2359304 | tf_op jit(solution)/shard_map/ppermute | solution.py:545
  10.3 48.8 %collective-permute-start.7 = (bf16[256,1536]{1,0:T(8,128)(2,1)}, bf16[256,1536]{1,0:T(8,128)(2,1)}, u32[]{:S(2)}, u32[]{:S(2)}) collective-permute-start(bf16[256,1536]{1,0:T(8,128)(2,1)} %refs_4_.1), channel_id=1, source_target_pairs={{0,16},{4,20},{8,24},{12,28},{16,0},{20,4},{24,8},{28,12},{1,17},{... | collective-permute-start | bytes 2359304 | tf_op jit(solution)/shard_map/ppermute | solution.py:545
  11.8 47.3 %collective-permute-start.11 = (bf16[512,256]{1,0:T(8,128)(2,1)}, bf16[512,256]{1,0:T(8,128)(2,1)}, u32[]{:S(2)}, u32[]{:S(2)}) collective-permute-start(bf16[512,256]{1,0:T(8,128)(2,1)} %refs_2_.1), channel_id=1, source_target_pairs={{0,4},{4,0},{8,12},{12,8},{16,20},{20,16},{24,28},{28,24},{1,5},{5... | collective-permute-start | bytes 786440 | tf_op jit(solution)/shard_map/ppermute | solution.py:545
  11.8 39.9 %collective-permute-start.12 = (bf16[512,256]{1,0:T(8,128)(2,1)}, bf16[512,256]{1,0:T(8,128)(2,1)S(1)}, u32[]{:S(2)}, u32[]{:S(2)}) collective-permute-start(bf16[512,256]{1,0:T(8,128)(2,1)} %refs_2_.1), channel_id=1, source_target_pairs={{0,8},{4,12},{8,0},{12,4},{16,24},{20,28},{24,16},{28,20},{1,9},{5... | collective-permute-start | bytes 786440 | tf_op jit(solution)/shard_map/ppermute | solution.py:545
  51.7 32.1 %collective-permute-start.19 = (bf16[256,2048]{1,0:T(8,128)(2,1)}, bf16[256,2048]{1,0:T(8,128)(2,1)S(1)}, u32[]{:S(2)}, u32[]{:S(2)}) collective-permute-start(bf16[256,2048]{1,0:T(8,128)(2,1)} %refs_12_.1), channel_id=1, source_target_pairs={{0,8},{4,12},{8,0},{12,4},{16,24},{20,28},{24,16},{28,20},{1,9},{5... | collective-permute-start | bytes 3145736 | tf_op jit(solution)/shard_map/ppermute | solution.py:545
  59.1 54.0 %collective-permute-start.26 = (bf16[2048,256]{1,0:T(8,128)(2,1)}, bf16[2048,256]{1,0:T(8,128)(2,1)}, u32[]{:S(2)}, u32[]{:S(2)}) collective-permute-start(bf16[2048,256]{1,0:T(8,128)(2,1)} %refs_1_.6), channel_id=1, source_target_pairs={{0,8},{4,12},{8,0},{12,4},{16,24},{20,28},{24,16},{28,20},{1,9},{5... | collective-permute-start | bytes 3145736 | tf_op jit(solution)/shard_map/ppermute | solution.py:545
  62.0 51.1 %collective-permute-start.28 = (bf16[2048,256]{1,0:T(8,128)(2,1)}, bf16[2048,256]{1,0:T(8,128)(2,1)}, u32[]{:S(2)}, u32[]{:S(2)}) collective-permute-start(bf16[2048,256]{1,0:T(8,128)(2,1)} %refs_1_.6), channel_id=1, source_target_pairs={{0,16},{4,20},{8,24},{12,28},{16,0},{20,4},{24,8},{28,12},{1,17},{... | collective-permute-start | bytes 3145736 | tf_op jit(solution)/shard_map/ppermute | solution.py:545
  85.6 35.4 %collective-permute-start.23 = (bf16[256,2048]{1,0:T(8,128)(2,1)}, bf16[256,2048]{1,0:T(8,128)(2,1)}, u32[]{:S(2)}, u32[]{:S(2)}) collective-permute-start(bf16[256,2048]{1,0:T(8,128)(2,1)} %broadcast_select_fusion.1), channel_id=1, source_target_pairs={{0,8},{4,20},{8,0},{12,28},{16,24},{20,4},{24,16},{28,12},{1,9},{5... | collective-permute-start | bytes 3145736 | tf_op jit(solution)/shard_map/ppermute | solution.py:551
  118.5 40.7 %collective-permute-start.18 = (bf16[256,2048]{1,0:T(8,128)(2,1)}, bf16[256,2048]{1,0:T(8,128)(2,1)}, u32[]{:S(2)}, u32[]{:S(2)}) collective-permute-start(bf16[256,2048]{1,0:T(8,128)(2,1)} %refs_12_.1), channel_id=1, source_target_pairs={{0,4},{4,0},{8,12},{12,8},{16,20},{20,16},{24,28},{28,24},{1,5},{5... | collective-permute-start | bytes 3145736 | tf_op jit(solution)/shard_map/ppermute | solution.py:545
  118.6 40.7 %collective-permute-start.20 = (bf16[256,2048]{1,0:T(8,128)(2,1)S(1)}, bf16[256,2048]{1,0:T(8,128)(2,1)}, u32[]{:S(2)}, u32[]{:S(2)}) collective-permute-start(bf16[256,2048]{1,0:T(8,128)(2,1)S(1)} %collective-permute-done.19.refs_3_.refs_14_), channel_id=1, source_target_pairs={{0,4},{4,0},{8,12},{12,8},{16,20},{20,16},{24,28},{28,24},{1,5},{5... | collective-permute-start | bytes 3145736 | tf_op jit(solution)/shard_map/ppermute | solution.py:545
  119.1 40.7 %collective-permute-start.22 = (bf16[256,2048]{1,0:T(8,128)(2,1)S(1)}, bf16[256,2048]{1,0:T(8,128)(2,1)}, u32[]{:S(2)}, u32[]{:S(2)}) collective-permute-start(bf16[256,2048]{1,0:T(8,128)(2,1)S(1)} %collective-permute-done.21.refs_5_.refs_16_), channel_id=1, source_target_pairs={{0,4},{4,0},{8,12},{12,8},{16,20},{20,16},{24,28},{28,24},{1,5},{5... | collective-permute-start | bytes 3145736 | tf_op jit(solution)/shard_map/ppermute | solution.py:545
  121.0 38.9 %collective-permute-start.30 = (bf16[2048,256]{1,0:T(8,128)(2,1)}, bf16[2048,256]{1,0:T(8,128)(2,1)}, u32[]{:S(2)}, u32[]{:S(2)}) collective-permute-start(bf16[2048,256]{1,0:T(8,128)(2,1)} %broadcast_select_fusion), channel_id=1, source_target_pairs={{0,8},{4,20},{8,0},{12,28},{16,24},{20,4},{24,16},{28,12},{1,9},{5... | collective-permute-start | bytes 3145736 | tf_op jit(solution)/shard_map/ppermute | solution.py:551
  138.2 33.7 %collective-permute-start.24 = (bf16[256,2048]{1,0:T(8,128)(2,1)}, bf16[256,2048]{1,0:T(8,128)(2,1)S(1)}, u32[]{:S(2)}, u32[]{:S(2)}) collective-permute-start(bf16[256,2048]{1,0:T(8,128)(2,1)} %collective-permute-done.23.refs_7_.refs_18_), channel_id=1, source_target_pairs={{0,4},{4,0},{8,12},{12,8},{16,20},{20,16},{24,28},{28,24},{1,5},{5... | collective-permute-start | bytes 3145736 | tf_op jit(solution)/shard_map/ppermute | solution.py:545
  159.2 30.4 %collective-permute-start.25 = (bf16[2048,256]{1,0:T(8,128)(2,1)S(1)}, bf16[2048,256]{1,0:T(8,128)(2,1)S(1)}, u32[]{:S(2)}, u32[]{:S(2)}) collective-permute-start(bf16[2048,256]{1,0:T(8,128)(2,1)S(1)} %copy-done.25), channel_id=1, source_target_pairs={{0,4},{4,0},{8,12},{12,8},{16,20},{20,16},{24,28},{28,24},{1,5},{5... | collective-permute-start | bytes 3145736 | tf_op jit(solution)/shard_map/ppermute | solution.py:545
  159.3 30.3 %collective-permute-start.27 = (bf16[2048,256]{1,0:T(8,128)(2,1)}, bf16[2048,256]{1,0:T(8,128)(2,1)S(1)}, u32[]{:S(2)}, u32[]{:S(2)}) collective-permute-start(bf16[2048,256]{1,0:T(8,128)(2,1)} %collective-permute-done.26.refs_12_.refs_3_), channel_id=1, source_target_pairs={{0,4},{4,0},{8,12},{12,8},{16,20},{20,16},{24,28},{28,24},{1,5},{5... | collective-permute-start | bytes 3145736 | tf_op jit(solution)/shard_map/ppermute | solution.py:545
  159.8 29.8 %collective-permute-start.29 = (bf16[2048,256]{1,0:T(8,128)(2,1)}, bf16[2048,256]{1,0:T(8,128)(2,1)S(1)}, u32[]{:S(2)}, u32[]{:S(2)}) collective-permute-start(bf16[2048,256]{1,0:T(8,128)(2,1)} %collective-permute-done.28.refs_14_.refs_5_), channel_id=1, source_target_pairs={{0,4},{4,0},{8,12},{12,8},{16,20},{20,16},{24,28},{28,24},{1,5},{5... | collective-permute-start | bytes 3145736 | tf_op jit(solution)/shard_map/ppermute | solution.py:545
  159.9 29.8 %collective-permute-start.31 = (bf16[2048,256]{1,0:T(8,128)(2,1)}, bf16[2048,256]{1,0:T(8,128)(2,1)S(1)}, u32[]{:S(2)}, u32[]{:S(2)}) collective-permute-start(bf16[2048,256]{1,0:T(8,128)(2,1)} %collective-permute-done.30.refs_16_.refs_7_), channel_id=1, source_target_pairs={{0,4},{4,0},{8,12},{12,8},{16,20},{20,16},{24,28},{28,24},{1,5},{5... | collective-permute-start | bytes 3145736 | tf_op jit(solution)/shard_map/ppermute | solution.py:545
  208.5 321.1 %reduce-scatter.5.cloned.1.call-start = ((), (), s32[]{:S(2)}) async-start(), calls=%async_computation.3 | async-start | bytes 28311552 | tf_op jit(solution)/shard_map/reduce_scatter | solution.py:748
  344.7 32.4 %collective-permute-start.46 = (bf16[128,2048]{1,0:T(8,128)(2,1)}, bf16[128,2048]{1,0:T(8,128)(2,1)S(1)}, u32[]{:S(2)}, u32[]{:S(2)}) collective-permute-start(bf16[128,2048]{1,0:T(8,128)(2,1)} %get-tuple-element.84), channel_id=1, source_target_pairs={{0,1},{1,2},{4,5},{5,6},{8,9},{9,10},{12,13},{13,14},{16,17},{17,1... | collective-permute-start | bytes 1572872 | tf_op jit(solution)/shard_map/ppermute | solution.py:620
  357.2 30.9 %collective-permute-start.42 = (bf16[128,2048]{1,0:T(8,128)(2,1)}, bf16[128,2048]{1,0:T(8,128)(2,1)S(1)}, u32[]{:S(2)}, u32[]{:S(2)}) collective-permute-start(bf16[128,2048]{1,0:T(8,128)(2,1)} %get-tuple-element.80), channel_id=1, source_target_pairs={{0,1},{1,2},{2,3},{4,5},{5,6},{6,7},{8,9},{9,10},{10,11},{12,13},{... | collective-permute-start | bytes 1572872 | tf_op jit(solution)/shard_map/ppermute | solution.py:620
  404.9 30.7 %collective-permute-start.34 = (bf16[256,2048]{1,0:T(8,128)(2,1)}, bf16[256,2048]{1,0:T(8,128)(2,1)S(1)}, u32[]{:S(2)}, u32[]{:S(2)}) collective-permute-start(bf16[256,2048]{1,0:T(8,128)(2,1)} %shard_map.269), channel_id=1, source_target_pairs={{0,1},{1,2},{2,3},{4,5},{5,6},{6,7},{8,9},{9,10},{10,11},{12,13},{... | collective-permute-start | bytes 3145736 | tf_op jit(solution)/shard_map/ppermute | solution.py:632
  422.8 38.1 %collective-permute-start.32 = (bf16[256,2048]{1,0:T(8,128)(2,1)S(1)}, bf16[256,2048]{1,0:T(8,128)(2,1)S(1)}, u32[]{:S(2)}, u32[]{:S(2)}) collective-permute-start(bf16[256,2048]{1,0:T(8,128)(2,1)S(1)} %copy-done), channel_id=1, source_target_pairs={{3,2},{2,1},{1,0},{7,6},{6,5},{5,4},{11,10},{10,9},{9,8},{15,14},{... | collective-permute-start | bytes 3145736 | tf_op jit(solution)/shard_map/ppermute | solution.py:633
  435.6 39.3 %collective-permute-start.35 = (bf16[256,2048]{1,0:T(8,128)(2,1)S(1)}, bf16[256,2048]{1,0:T(8,128)(2,1)S(1)}, u32[]{:S(2)}, u32[]{:S(2)}) collective-permute-start(bf16[256,2048]{1,0:T(8,128)(2,1)S(1)} %collective-permute-done.34), channel_id=1, source_target_pairs={{1,2},{2,3},{5,6},{6,7},{9,10},{10,11},{13,14},{14,15},{17,18},{18... | collective-permute-start | bytes 3145736 | tf_op jit(solution)/shard_map/ppermute | solution.py:632
  443.2 28.8 %collective-permute-start.55 = (bf16[128,2048]{1,0:T(8,128)(2,1)S(1)}, bf16[128,2048]{1,0:T(8,128)(2,1)S(1)}, u32[]{:S(2)}, u32[]{:S(2)}) collective-permute-start(bf16[128,2048]{1,0:T(8,128)(2,1)S(1)} %collective-permute-done.54), channel_id=1, source_target_pairs={{2,1},{1,0},{6,5},{5,4},{10,9},{9,8},{14,13},{13,12},{18,17},{17,1... | collective-permute-start | bytes 1572872 | tf_op jit(solution)/shard_map/ppermute | solution.py:633
  444.5 28.8 %collective-permute-start.57 = (bf16[128,2048]{1,0:T(8,128)(2,1)S(1)}, bf16[128,2048]{1,0:T(8,128)(2,1)}, u32[]{:S(2)}, u32[]{:S(2)}) collective-permute-start(bf16[128,2048]{1,0:T(8,128)(2,1)S(1)} %collective-permute-done.56), channel_id=1, source_target_pairs={{1,2},{2,3},{5,6},{6,7},{9,10},{10,11},{13,14},{14,15},{17,18},{18... | collective-permute-start | bytes 1572872 | tf_op jit(solution)/shard_map/ppermute | solution.py:632
  447.9 86.6 %collective-permute-start.58 = (bf16[128,2048]{1,0:T(8,128)(2,1)}, bf16[128,2048]{1,0:T(8,128)(2,1)}, u32[]{:S(2)}, u32[]{:S(2)}) collective-permute-start(bf16[128,2048]{1,0:T(8,128)(2,1)} %collective-permute-done.53), channel_id=1, source_target_pairs={{2,3},{6,7},{10,11},{14,15},{18,19},{22,23},{26,27},{30,31}} | collective-permute-start | bytes 1572872 | tf_op jit(solution)/shard_map/ppermute | solution.py:632
  460.8 33.7 %collective-permute-start.33 = (bf16[256,2048]{1,0:T(8,128)(2,1)S(1)}, bf16[256,2048]{1,0:T(8,128)(2,1)S(1)}, u32[]{:S(2)}, u32[]{:S(2)}) collective-permute-start(bf16[256,2048]{1,0:T(8,128)(2,1)S(1)} %collective-permute-done.32), channel_id=1, source_target_pairs={{2,1},{1,0},{6,5},{5,4},{10,9},{9,8},{14,13},{13,12},{18,17},{17,1... | collective-permute-start | bytes 3145736 | tf_op jit(solution)/shard_map/ppermute | solution.py:633
  472.0 66.6 %collective-permute-start.60 = (bf16[128,2048]{1,0:T(8,128)(2,1)}, bf16[128,2048]{1,0:T(8,128)(2,1)}, u32[]{:S(2)}, u32[]{:S(2)}) collective-permute-start(bf16[128,2048]{1,0:T(8,128)(2,1)} %collective-permute-done.51), channel_id=1, source_target_pairs={{1,0},{5,4},{9,8},{13,12},{17,16},{21,20},{25,24},{29,28}} | collective-permute-start | bytes 1572872 | tf_op jit(solution)/shard_map/ppermute | solution.py:633
  473.3 63.3 %collective-permute-start.59 = (bf16[128,2048]{1,0:T(8,128)(2,1)}, bf16[128,2048]{1,0:T(8,128)(2,1)}, u32[]{:S(2)}, u32[]{:S(2)}) collective-permute-start(bf16[128,2048]{1,0:T(8,128)(2,1)} %collective-permute-done.57), channel_id=1, source_target_pairs={{2,3},{6,7},{10,11},{14,15},{18,19},{22,23},{26,27},{30,31}} | collective-permute-start | bytes 1572872 | tf_op jit(solution)/shard_map/ppermute | solution.py:632
  494.5 33.7 %collective-permute-start.37 = (bf16[256,2048]{1,0:T(8,128)(2,1)S(1)}, bf16[256,2048]{1,0:T(8,128)(2,1)S(1)}, u32[]{:S(2)}, u32[]{:S(2)}) collective-permute-start(bf16[256,2048]{1,0:T(8,128)(2,1)S(1)} %collective-permute-done.33), channel_id=1, source_target_pairs={{1,0},{5,4},{9,8},{13,12},{17,16},{21,20},{25,24},{29,28}} | collective-permute-start | bytes 3145736 | tf_op jit(solution)/shard_map/ppermute | solution.py:633
  497.2 43.5 %collective-permute-start.61 = (bf16[128,2048]{1,0:T(8,128)(2,1)S(1)}, bf16[128,2048]{1,0:T(8,128)(2,1)S(1)}, u32[]{:S(2)}, u32[]{:S(2)}) collective-permute-start(bf16[128,2048]{1,0:T(8,128)(2,1)S(1)} %collective-permute-done.55), channel_id=1, source_target_pairs={{1,0},{5,4},{9,8},{13,12},{17,16},{21,20},{25,24},{29,28}} | collective-permute-start | bytes 1572872 | tf_op jit(solution)/shard_map/ppermute | solution.py:633
  (72 other events, 1227.8 us)
Sparse Core Ops, SparseCore 0:
  208.6 76.8 reduce-scatter.2
  289.1 157.5 reduce-scatter.4
